TPU v7x, 128 devices: a whole 4x4x4 slice. The times are simulated.
128 devices in a mesh: rep: 8 (over z, core), tensor: 16 (over y, x).
Axes of the slice: x: 4, y: 4, z: 4, core: 2. Of those that a mesh axis runs over, the one named last changes fastest.
Arguments:
- x_pre: bfloat16 [8192, 2560], P(('rep', 'tensor')), may hold values from -6 to 6
- x_dec: bfloat16 [16, 2560], replicated, may hold values from -6 to 6
- prefix_kv: bfloat16 [8, 4096, 32, 160], P('rep', None, 'tensor'), may hold values from -400 to 400
- cache_kv: bfloat16 [16, 4096, 32, 160], P(None, 'rep', 'tensor'), may hold values from -400 to 400
- dec_len: int32 [16], replicated, may hold values from 1 to 4096, as said below
- offsets: int32 [8], P('rep'), may hold values from 0 to 4096, as said below
- segments: int32 [8, 1024], P('rep'), may hold values from 0 to 3, never falling along the last dimension, each value on 1 to 512 neighbouring positions
- w_qkv: bfloat16 [2560, 7680], P(None, 'tensor'), may hold values from -0.125 to 0.125
- w_out: bfloat16 [2560, 2560], P('tensor'), may hold values from -0.125 to 0.125
- w_up: bfloat16 [2560, 10240], P(None, 'tensor'), may hold values from -0.125 to 0.125
- up_bias: float32 [10240], P('tensor'), may hold values from -3 to 3
- w_down: bfloat16 [10240, 2560], P('tensor'), may hold values from -0.0625 to 0.0625
- biases: float32 [2, 2560], replicated, may hold values from -3 to 3
- gains: float32 [2, 2560], replicated, may hold values from 0.1 to 1.9
- shifts: float32 [2, 2560], replicated, may hold values from -2.5 to 2.5
- w_next: bfloat16 [2560, 7680], P(None, 'tensor'), may hold values from -0.125 to 0.125
Outputs:
- layer_out: bfloat16 [8192, 2560], P(('rep', 'tensor'))
- next_qkv: bfloat16 [8192, 7680], P('rep', 'tensor')
- dec_out: bfloat16 [16, 2560], replicated
- dec_next_qkv: bfloat16 [16, 7680], P(None, 'tensor')
Inputs may be any that keep to these rules, and one draw needn't show every extreme that they name: Request r's cache holds live entries at positions below dec_len[r]; in every draw one request's cache is full (4096) and one request has a single live position. `offsets`: in every draw one span has a full earlier cache (4096 positions) and one span has none.
All inputs are finite; a program needn't handle non-finite values.
Results may differ from a plain program's by a relative error of at most 0.025.
Values may be sent and summed in bfloat16 or wider, within the bound.
A program may use at most 192 MiB of HBM per device.

v0:
```python
import jax
import jax.numpy as jnp
from jax import lax
from jax.sharding import PartitionSpec as P

NEG = -1e30


def combined_all(value, axis, join):
    pieces = jax.tree.map(lambda part: lax.all_gather(part, axis), value)
    head = jax.tree.map(lambda part: part[0], pieces)
    tail = jax.tree.map(lambda part: part[1:], pieces)
    total, _ = lax.scan(lambda total, slab: (join(total, slab), None), head, tail)
    return total


def layer_norm(values, gain_row, shift_row):
    average = jnp.mean(values, axis=-1, keepdims=True)
    centred = values - average
    spread = jnp.mean(centred * centred, axis=-1, keepdims=True)
    return centred * lax.rsqrt(spread + 1e-05) * gain_row + shift_row


def visible(seg_query, query_pos, seg_all, offset, prefix_len):
    prefix_pos = jnp.arange(prefix_len)
    from_prefix = (prefix_pos[None, :] < offset) & (seg_query[:, None] == 0)
    span_pos = jnp.arange(seg_all.shape[0])
    from_span = (seg_all[None, :] == seg_query[:, None]) & (span_pos[None, :] <= query_pos[:, None])
    return jnp.concatenate([from_prefix, from_span], axis=1)


def combine(earlier, later):
    high_early, total_early, output_early = earlier
    high_later, total_later, output_later = later
    highest = jnp.maximum(high_early, high_later)
    factor_early = jnp.exp(high_early - highest)
    factor_later = jnp.exp(high_later - highest)
    return (
        highest,
        total_early * factor_early + total_later * factor_later,
        output_early * factor_early[..., None] + output_later * factor_later[..., None],
    )


def block_state(queries, keys, values, valid, scale):
    scores = jnp.einsum("rhd,rphd->rhp", queries, keys, preferred_element_type=jnp.float32) * scale
    scores = jnp.where(valid[:, None, :], scores, NEG)
    highest = jnp.max(scores, axis=-1)
    weights = jnp.where(valid[:, None, :], jnp.exp(scores - highest[..., None]), 0.0)
    totals = jnp.sum(weights, axis=-1)
    output = jnp.einsum("rhp,rphd->rhd", weights, values.astype(jnp.float32))
    return (highest, totals, output)


def per_device(
    x_pre,
    x_dec,
    prefix_kv,
    cache_kv,
    dec_len,
    offsets,
    segments,
    w_qkv,
    w_out,
    w_up,
    up_bias,
    w_down,
    biases,
    gains,
    shifts,
    w_next,
):
    heads_dev = prefix_kv.shape[2]
    head_dim = prefix_kv.shape[3] // 2
    prefix_len = prefix_kv.shape[1]
    span_len = segments.shape[1]
    scale = head_dim ** (-0.5)

    def up_rows(piece):
        return jax.nn.gelu(
            jnp.dot(piece, w_up, preferred_element_type=jnp.float32) + up_bias, approximate=False
        ).astype(jnp.bfloat16)

    def next_rows(piece):
        return jnp.dot(piece, w_next, preferred_element_type=jnp.float32).astype(jnp.bfloat16)

    qkv_all = jnp.dot(
        lax.all_gather(x_pre, "tensor", axis=0, tiled=True),
        w_qkv,
        preferred_element_type=jnp.float32,
    ).astype(jnp.bfloat16)
    dec_qkv = jnp.dot(x_dec, w_qkv, preferred_element_type=jnp.float32).astype(jnp.bfloat16)
    dec_four = dec_qkv.reshape(dec_qkv.shape[0], heads_dev, 3, head_dim)
    dec_query = dec_four[:, :, 0]
    positions = cache_kv.shape[1]
    cache_base = lax.axis_index("rep") * positions
    valid = (cache_base + jnp.arange(positions))[None, :] < dec_len[:, None]
    state = block_state(dec_query, cache_kv[..., :head_dim], cache_kv[..., head_dim:], valid, scale)
    is_first = lax.axis_index("rep") == 0
    own_score = (
        jnp.sum(dec_query.astype(jnp.float32) * dec_four[:, :, 1].astype(jnp.float32), axis=-1)
        * scale
    )
    own_state = (
        jnp.where(is_first, own_score, NEG),
        jnp.where(is_first, jnp.ones_like(own_score), jnp.zeros_like(own_score)),
        jnp.where(is_first, dec_four[:, :, 2].astype(jnp.float32), 0.0),
    )
    state = combine(state, own_state)
    merged = combined_all(state, "rep", combine)
    dec_attn = (
        (merged[2] / merged[1][..., None])
        .astype(jnp.bfloat16)
        .reshape(dec_qkv.shape[0], heads_dev * head_dim)
    )
    qkv_four = qkv_all.reshape(span_len, heads_dev, 3, head_dim)
    queries = qkv_four[:, :, 0]
    prefix = prefix_kv[0]
    keys = jnp.concatenate([prefix[:, :, :head_dim], qkv_four[:, :, 1]], axis=0)
    values = jnp.concatenate([prefix[:, :, head_dim:], qkv_four[:, :, 2]], axis=0)
    seg_all = segments[0]
    offset = offsets[0]
    query_block = min(512, span_len)

    def attend_block(index):
        begin = index * query_block
        query_rows = lax.dynamic_slice_in_dim(queries, begin, query_block, 0)
        seg_query = lax.dynamic_slice_in_dim(seg_all, begin, query_block, 0)
        mask = visible(seg_query, begin + jnp.arange(query_block), seg_all, offset, prefix_len)
        scores = (
            jnp.einsum("qhd,khd->hqk", query_rows, keys, preferred_element_type=jnp.float32) * scale
        )
        scores = jnp.where(mask[None], scores, NEG)
        highest = jnp.max(scores, axis=-1, keepdims=True)
        weights = jnp.where(mask[None], jnp.exp(scores - highest), 0.0)
        weights = (weights / jnp.sum(weights, axis=-1, keepdims=True)).astype(jnp.bfloat16)
        return jnp.einsum(
            "hqk,khd->qhd", weights, values, preferred_element_type=jnp.float32
        ).astype(jnp.bfloat16)

    blocks = lax.map(attend_block, jnp.arange(span_len // query_block))
    attn = blocks.reshape(span_len, heads_dev * head_dim)
    attn_part = lax.psum_scatter(
        jnp.dot(attn, w_out, preferred_element_type=jnp.float32).astype(jnp.bfloat16),
        "tensor",
        scatter_dimension=0,
        tiled=True,
    ).astype(jnp.float32)
    dec_sum = lax.psum(
        jnp.dot(dec_attn, w_out, preferred_element_type=jnp.float32).astype(jnp.bfloat16), "tensor"
    ).astype(jnp.float32)
    h_first = layer_norm(
        x_pre.astype(jnp.float32) + attn_part + biases[0], gains[0], shifts[0]
    ).astype(jnp.bfloat16)
    hidden = up_rows(lax.all_gather(h_first, "tensor", axis=0, tiled=True))
    dec_first = layer_norm(
        x_dec.astype(jnp.float32) + dec_sum + biases[0], gains[0], shifts[0]
    ).astype(jnp.bfloat16)
    mlp_part = lax.psum_scatter(
        jnp.dot(hidden, w_down, preferred_element_type=jnp.float32).astype(jnp.bfloat16),
        "tensor",
        scatter_dimension=0,
        tiled=True,
    ).astype(jnp.float32)
    layer_out = layer_norm(
        h_first.astype(jnp.float32) + mlp_part + biases[1], gains[1], shifts[1]
    ).astype(jnp.bfloat16)
    dec_hidden = up_rows(dec_first)
    dec_mlp = lax.psum(
        jnp.dot(dec_hidden, w_down, preferred_element_type=jnp.float32).astype(jnp.bfloat16),
        "tensor",
    ).astype(jnp.float32)
    dec_out = layer_norm(
        dec_first.astype(jnp.float32) + dec_mlp + biases[1], gains[1], shifts[1]
    ).astype(jnp.bfloat16)
    next_qkv = next_rows(lax.all_gather(layer_out, "tensor", axis=0, tiled=True))
    dec_next_qkv = next_rows(dec_out)
    return (layer_out, next_qkv, dec_out, dec_next_qkv)


def solution(mesh):
    placed = (
        P(("rep", "tensor"), None),
        P(),
        P("rep", None, "tensor", None),
        P(None, "rep", "tensor", None),
        P(),
        P("rep"),
        P("rep", None),
        P(None, "tensor"),
        P("tensor", None),
        P(None, "tensor"),
        P("tensor"),
        P("tensor", None),
        P(),
        P(),
        P(),
        P(None, "tensor"),
    )
    return jax.shard_map(
        per_device,
        mesh=mesh,
        in_specs=placed,
        out_specs=(P(("rep", "tensor"), None), P("rep", "tensor"), P(), P(None, "tensor")),
        check_vma=False,
    )
```

profile of v0, /device:TPU:0, one launch (start us, length us, event | category | flops | bytes accessed | tf_op | source)
XLA Modules:
  0.0 647.6 jit_solution(16715024463593659003)
XLA Ops:
  8.0 3.7 fusion.182
  11.7 57.2 %all-gather.5.cloned.1.call-done = bf16[1024,2560]{1,0:T(8,128)(2,1)} async-done(((bf16[64,2560]{1,0:T(8,128)(2,1)}), bf16[1024,2560]{1,0:T(8,128)(2,1)}) %all-gather.5.cloned.1.call-update) | async-done | bytes 5242896 | tf_op jit(solution)/shard_map/all_gather | solution.py:88
  68.9 6.1 convolution_convert_fusion.5
  76.4 2.0 pad_maximum_fusion
  78.4 101.0 %while.24 = (s32[]{:T(128)}, bf16[2,512,2,80]{1,3,2,0:T(8,128)(2,1)}, s32[]{:T(128)}, s32[2]{0:T(128)S(1)}, s32[1024]{0:T(1024)S(1)}, /*index=5*/s32[1,1024]{1,0...) while((s32[]{:T(128)}, ...), condition=%wide.region_3.4_spmd, body=%wide.region_0.3_spmd.sunk | while | flops 1731291136 | bytes 107183400 | solution.py:141
  79.7 11.4 %fusion.215 = f32[2,512,5120]{2,1,0:T(8,128)} fusion(bf16[5120,2,80]{0,2,1:T(8,128)(2,1)} %get-tuple-element.300, bf16[1024,2,80]{0,2,1:T(8,128)(2,1)} %get-tuple-element.299, s32[]{:T(128)S(6)} %select_n.124), kind=kOutput, calls=%fused_computation.16.clone.1 | convolution fusion | flops 838860800 | bytes 22773764 | tf_op jit(solution)/shard_map/while/body/eval_jaxpr/qhd,khd->hqk/dot_general | solution.py:131
  93.9 25.4 %fusion.217 = (f32[2,512]{1,0:T(2,128)S(1)}, f32[2,512,5120]{2,1,0:T(8,128)}) fusion(f32[2,512,5120]{2,1,0:T(8,128)} %fusion.215, pred[512,5120]{1,0:T(8,128)(4,1)S(1)} %pad_add_fusion.2), kind=kOutput, calls=%fused_computation.273.clone.1 | output fusion | flops 36705280 | bytes 44568576 | tf_op jit(solution)/shard_map/while/body/eval_jaxpr/sub | solution.py:135
  119.3 8.8 %fusion.218 = bf16[2,512,2,80]{1,3,2,0:T(8,128)(2,1)S(1)} fusion(bf16[2,512,2,80]{1,3,2,0:T(8,128)(2,1)S(1)} %copy-done.6, s32[]{:T(128)S(6)} %copy.93, bf16[5120,2,80]{0,2,1:T(8,128)(2,1)S(1)} %copy-done.3, f32[2,512,5120]{2,1,0:T(8,128)} %get-tuple-element.254, f32[2,512]{1,0:T(2,128)S(1)} %get-tuple-element.255), kind=kOutput, calls=%fused_computation.15.clone.1 | convolution fusion | flops 849428480 | bytes 22777860 | tf_op jit(solution)/shard_map/while/body/eval_jaxpr/hqk,khd->qhd/dot_general | solution.py:137
  130.1 11.4 %fusion.215 = f32[2,512,5120]{2,1,0:T(8,128)} fusion(bf16[5120,2,80]{0,2,1:T(8,128)(2,1)} %get-tuple-element.300, bf16[1024,2,80]{0,2,1:T(8,128)(2,1)} %get-tuple-element.299, s32[]{:T(128)S(6)} %select_n.124), kind=kOutput, calls=%fused_computation.16.clone.1 | convolution fusion | flops 838860800 | bytes 22773764 | tf_op jit(solution)/shard_map/while/body/eval_jaxpr/qhd,khd->hqk/dot_general | solution.py:131
  144.4 25.4 %fusion.217 = (f32[2,512]{1,0:T(2,128)S(1)}, f32[2,512,5120]{2,1,0:T(8,128)}) fusion(f32[2,512,5120]{2,1,0:T(8,128)} %fusion.215, pred[512,5120]{1,0:T(8,128)(4,1)S(1)} %pad_add_fusion.2), kind=kOutput, calls=%fused_computation.273.clone.1 | output fusion | flops 36705280 | bytes 44568576 | tf_op jit(solution)/shard_map/while/body/eval_jaxpr/sub | solution.py:135
  169.8 8.8 %fusion.218 = bf16[2,512,2,80]{1,3,2,0:T(8,128)(2,1)S(1)} fusion(bf16[2,512,2,80]{1,3,2,0:T(8,128)(2,1)S(1)} %copy-done.6, s32[]{:T(128)S(6)} %copy.93, bf16[5120,2,80]{0,2,1:T(8,128)(2,1)S(1)} %copy-done.3, f32[2,512,5120]{2,1,0:T(8,128)} %get-tuple-element.254, f32[2,512]{1,0:T(2,128)S(1)} %get-tuple-element.255), kind=kOutput, calls=%fused_computation.15.clone.1 | convolution fusion | flops 849428480 | bytes 22777860 | tf_op jit(solution)/shard_map/while/body/eval_jaxpr/hqk,khd->qhd/dot_general | solution.py:137
  180.8 5.0 convolution_convert_fusion.1
  186.7 77.8 %reduce-scatter.3.cloned.1.call-done = bf16[64,2560]{1,0:T(8,128)(2,1)} async-done(((bf16[1024,2560]{1,0:T(8,128)(2,1)}), bf16[64,2560]{1,0:T(8,128)(2,1)}) %reduce-scatter.3.cloned.1.call-update) | async-done | bytes 327696 | tf_op jit(solution)/shard_map/reduce_scatter | solution.py:143
  267.2 2.0 add_convert_fusion.1
  269.5 2.5 convolution_convert_fusion.7
  272.9 2.2 fusion.23
  276.7 2.6 fusion.21
  279.5 13.2 %all-gather = f32[128,2,80]{2,1,0:T(2,128)S(1)} all-gather(f32[16,2,80]{2,1,0:T(2,128)S(1)} %multiply_add_fusion), channel_id=2, replica_groups=mesh['rep'=8,'tensor'=16] {'rep'}, dimensions={0}, use_global_device_ids=true | all-gather | bytes 92160 | tf_op jit(solution)/shard_map/all_gather | solution.py:10
  294.9 10.2 %all_gather.26 = f32[8,16,2]{1,2,0:T(2,128)S(1)} all-gather(f32[1,16,2]{1,2,0:T(2,128)S(1)} %get-tuple-element.148), channel_id=1, replica_groups=mesh['rep'=8,'tensor'=16] {'rep'}, dimensions={0}, use_global_device_ids=true | all-gather | bytes 1152 | tf_op jit(solution)/shard_map/all_gather | solution.py:10
  305.1 8.1 %all_gather.27 = f32[8,16,2]{1,2,0:T(2,128)S(1)} all-gather(f32[1,16,2]{1,2,0:T(2,128)S(1)} %get-tuple-element.147), channel_id=1, replica_groups=mesh['rep'=8,'tensor'=16] {'rep'}, dimensions={0}, use_global_device_ids=true | all-gather | bytes 1152 | tf_op jit(solution)/shard_map/all_gather | solution.py:10
  313.3 7.4 %while.25 = (s32[]{:T(128)}, f32[16,2]{0,1:T(2,128)S(1)}, f32[16,2]{0,1:T(2,128)S(1)}, f32[16,2,80]{2,1,0:T(2,128)S(1)}, f32[7,16,2]{1,2,0:T(2,128)S(1)}, /*inde...) while((s32[]{:T(128)}, f32[16,2]{0,1:T(2,128)S(1)}, f32[16,2]{0,1:T(2,128)S(1)}, ...), condition=%wide.region_14.15_spmd, body=%wide.region_13.14_spmd.sunk | while | flops 7874 | bytes 32613 | solution.py:13
  321.0 2.0 convolution_convert_fusion.3
  323.1 1.9 all-gather.7.cloned.1.call-done
  325.0 17.9 %convolution_convert_fusion = bf16[1024,2560]{1,0:T(8,128)(2,1)} fusion(bf16[640,2560]{1,0:T(8,128)(2,1)S(1)} %copy-done, bf16[1024,2560]{1,0:T(8,128)(2,1)} %all-gather.7.cloned.1.call-done, bf16[2560,640]{1,0:T(8,128)(2,1)} %param.29, f32[640]{0:T(1024)} %param.30), kind=kOutput, calls=%fused_computation.33 | convolution fusion | flops 6756761600 | bytes 17041920 | tf_op jit(solution)/shard_map/dot_general | solution.py:160
  343.0 66.2 %all-reduce.3.cloned.1.call-done = bf16[16,2560]{1,0:T(8,128)(2,1)} async-done(((bf16[16,2560]{1,0:T(8,128)(2,1)}), bf16[16,2560]{1,0:T(8,128)(2,1)}) %all-reduce.3.cloned.1.call-update) | async-done | bytes 81936 | tf_op jit(solution)/shard_map/psum | solution.py:149
  412.3 3.6 convolution_convert_fusion.2
  416.0 75.1 %reduce-scatter.5.cloned.1.call-done = bf16[64,2560]{1,0:T(8,128)(2,1)} async-done(((bf16[1024,2560]{1,0:T(8,128)(2,1)}), bf16[64,2560]{1,0:T(8,128)(2,1)}) %reduce-scatter.5.cloned.1.call-update) | async-done | bytes 327696 | tf_op jit(solution)/shard_map/reduce_scatter | solution.py:159
  493.7 2.0 add_convert_fusion
  495.8 79.6 %all-reduce.5.cloned.1.call-done = bf16[16,2560]{1,0:T(8,128)(2,1)} async-done(((bf16[16,2560]{1,0:T(8,128)(2,1)}), bf16[16,2560]{1,0:T(8,128)(2,1)}) %all-reduce.5.cloned.1.call-update) | async-done | bytes 81936 | tf_op jit(solution)/shard_map/psum | solution.py:169
  578.5 3.1 convolution_convert_fusion.6
  581.6 52.2 %all-gather.9.cloned.1.call-done = bf16[1024,2560]{1,0:T(8,128)(2,1)} async-done(((bf16[64,2560]{1,0:T(8,128)(2,1)}), bf16[1024,2560]{1,0:T(8,128)(2,1)}) %all-gather.9.cloned.1.call-update) | async-done | bytes 5242896 | tf_op jit(solution)/shard_map/all_gather | solution.py:176
  633.8 6.9 %convolution_convert_fusion.4 = bf16[1024,480]{0,1:T(8,128)(2,1)} fusion(bf16[1024,2560]{1,0:T(8,128)(2,1)} %all-gather.9.cloned.1.call-done, bf16[2560,480]{0,1:T(8,128)(2,1)} %param.35), kind=kOutput, calls=%fused_computation.62 | convolution fusion | flops 2517073920 | bytes 8683520 | tf_op jit(solution)/shard_map/dot_general | solution.py:85
  (148 shorter events, 37.0 us)
Async XLA Ops:
  7.2 317.8 %copy-start = (bf16[640,2560]{1,0:T(8,128)(2,1)S(1)}, bf16[640,2560]{1,0:T(8,128)(2,1)}, u32[]{:S(2)}) copy-start(bf16[640,2560]{1,0:T(8,128)(2,1)} %param.31) | copy-start | bytes 9830404
  7.2 61.7 %all-gather.5.cloned.1.call-start = ((), (), s32[]{:S(2)}) async-start(), calls=%async_computation.2 | async-start | bytes 5570560 | tf_op jit(solution)/shard_map/all_gather | solution.py:88
  7.9 256.6 %reduce-scatter.3.cloned.1.call-start = ((), (), s32[]{:S(2)}) async-start(), calls=%async_computation.3 | async-start | bytes 5570560 | tf_op jit(solution)/shard_map/reduce_scatter | solution.py:143
  68.9 6.9 %copy-start.2 = (bf16[4096,2,80]{0,2,1:T(8,128)(2,1)S(1)}, bf16[4096,2,80]{0,2,1:T(8,128)(2,1)}, u32[]{:S(2)}) copy-start(bf16[4096,2,80]{0,2,1:T(8,128)(2,1)} %get-tuple-element.139) | copy-start | bytes 3932164
  75.0 1.4 copy-start.1
  76.4 2.0 copy-start.8
  93.9 25.4 %copy-start.3 = (bf16[5120,2,80]{0,2,1:T(8,128)(2,1)S(1)}, bf16[5120,2,80]{0,2,1:T(8,128)(2,1)}, u32[]{:S(2)}) copy-start(bf16[5120,2,80]{0,2,1:T(8,128)(2,1)} %get-tuple-element.301) | copy-start | bytes 4915204 | tf_op jit(solution)/shard_map/while
  93.9 25.4 %copy-start.6 = (bf16[2,512,2,80]{1,3,2,0:T(8,128)(2,1)S(1)}, bf16[2,512,2,80]{1,3,2,0:T(8,128)(2,1)}, u32[]{:S(2)}) copy-start(bf16[2,512,2,80]{1,3,2,0:T(8,128)(2,1)} %get-tuple-element.281) | copy-start | bytes 983044 | tf_op jit(solution)/shard_map/while
  128.2 0.7 copy-start.7
  144.4 25.4 %copy-start.3 = (bf16[5120,2,80]{0,2,1:T(8,128)(2,1)S(1)}, bf16[5120,2,80]{0,2,1:T(8,128)(2,1)}, u32[]{:S(2)}) copy-start(bf16[5120,2,80]{0,2,1:T(8,128)(2,1)} %get-tuple-element.301) | copy-start | bytes 4915204 | tf_op jit(solution)/shard_map/while
  144.4 25.4 %copy-start.6 = (bf16[2,512,2,80]{1,3,2,0:T(8,128)(2,1)S(1)}, bf16[2,512,2,80]{1,3,2,0:T(8,128)(2,1)}, u32[]{:S(2)}) copy-start(bf16[2,512,2,80]{1,3,2,0:T(8,128)(2,1)} %get-tuple-element.281) | copy-start | bytes 983044 | tf_op jit(solution)/shard_map/while
  178.7 0.7 copy-start.7
  185.8 0.7 copy-start.12
  185.8 0.8 copy-start.13
  185.8 0.8 copy-start.14
  185.8 83.7 %copy-start.4 = (bf16[16,2560]{1,0:T(8,128)(2,1)S(1)}, bf16[16,2560]{1,0:T(8,128)(2,1)}, u32[]{:S(2)}) copy-start(bf16[16,2560]{1,0:T(8,128)(2,1)} %param.21) | copy-start | bytes 245764
  185.8 139.2 %all-gather.7.cloned.1.call-start = ((), (), s32[]{:S(2)}) async-start(), calls=%async_computation.4 | async-start | bytes 5570560 | tf_op jit(solution)/shard_map/all_gather | solution.py:155
  264.5 8.4 %copy-start.17 = (s32[16]{0:T(128)S(1)}, s32[16]{0:T(128)}, u32[]{:S(2)}) copy-start(s32[16]{0:T(128)} %param.24) | copy-start | bytes 196
  269.2 140.0 %all-reduce.3.cloned.1.call-start = ((), (), s32[]{:S(2)}) async-start(), calls=%async_computation.7 | async-start | bytes 163840 | tf_op jit(solution)/shard_map/psum | solution.py:149
  272.9 2.4 copy-start.15
  275.2 4.1 copy-start.11
  276.6 2.7 copy-start.9
  276.6 2.8 copy-start.10
  323.0 168.1 %reduce-scatter.5.cloned.1.call-start = ((), (), s32[]{:S(2)}) async-start(), calls=%async_computation.5 | async-start | bytes 5570560 | tf_op jit(solution)/shard_map/reduce_scatter | solution.py:159
  342.9 69.4 %copy-start.16 = (f32[640]{0:T(1024)S(1)}, f32[640]{0:T(1024)}, u32[]{:S(2)}) copy-start(f32[640]{0:T(1024)} %param.30) | copy-start | bytes 7684
  343.0 232.4 %all-reduce.5.cloned.1.call-start = ((), (), s32[]{:S(2)}) async-start(), calls=%async_computation.8 | async-start | bytes 163840 | tf_op jit(solution)/shard_map/psum | solution.py:169
  415.9 217.8 %all-gather.9.cloned.1.call-start = ((), (), s32[]{:S(2)}) async-start(), calls=%async_computation.6 | async-start | bytes 5570560 | tf_op jit(solution)/shard_map/all_gather | solution.py:176
  578.5 62.2 %copy-start.5 = (bf16[16,2560]{1,0:T(8,128)(2,1)}, bf16[16,2560]{1,0:T(8,128)(2,1)S(1)}, u32[]{:S(2)}) copy-start(bf16[16,2560]{1,0:T(8,128)(2,1)S(1)} %add_convert_fusion.2) | copy-start | bytes 245764
Sparse Core Ops, SparseCore 0:
  10.2 58.7 all-gather.4
  185.9 78.5 reduce-scatter.2
  269.3 55.6 all-gather.6
  328.7 80.4 all-reduce.2
  412.7 78.2 reduce-scatter.4
  495.1 80.2 all-reduce.4
  578.0 55.6 all-gather.8
where the time goes:
time: 650 us; the launch traced here: 648 us
  waiting for transfers between devices  411 us (63%)
  matrix products  92.5 us (14%)
  other arithmetic  82.2 us (13%)
  blocking collectives  31.6 us (5%)
  between operations  14.4 us (2%)
  local copies, waits for them, and re-layouts  14.1 us (2%)
    psum x1, waiting for transfers between devices, per_device(): lax.psum(jnp.dot(dec_hidden, w_down, preferred_element_type=jnp.float32)....  79.6 us
    reduce_scatter x1, waiting for transfers between devices, per_device(): lax.psum_scatter(jnp.dot(attn, w_out, preferred_element_type=jnp.float32)...  77.8 us
    reduce_scatter x1, waiting for transfers between devices, per_device(): lax.psum_scatter(jnp.dot(hidden, w_down, preferred_element_type=jnp.float...  75.1 us
    psum x1, waiting for transfers between devices, per_device(): lax.psum(jnp.dot(dec_attn, w_out, preferred_element_type=jnp.float32).ast...  66.2 us
    all_gather x1, waiting for transfers between devices, per_device(): lax.all_gather(x_pre, 'tensor', axis=0, tiled=True)  57.2 us
    all_gather x1, waiting for transfers between devices, per_device(): lax.all_gather(layer_out, 'tensor', axis=0, tiled=True)  52.2 us
    sub x2, other arithmetic, attend_block(): weights = jnp.where(mask[None], jnp.exp(scores - highest), 0.0)  50.8 us
    all_gather x3, blocking collectives, combined_all(): pieces = jax.tree.map(lambda part: lax.all_gather(part, axis), value)  31.6 us
  transfers between devices with their start and end apart: 7, of which 7 were waited for; matrix products, arithmetic and copies ran while one was open for 9% of the time, Pallas kernels for 0%

commit v1 on v0

v1 whole, which is shorter than its diff:
```python
import functools

import jax
import jax.numpy as jnp
from jax import lax
from jax.experimental import pallas as pl
from jax.experimental.pallas import tpu as pltpu
from jax.sharding import PartitionSpec as P

MESH = pl.DeviceIdType.MESH
NEG = -1e30
LOG2E = 1.4426950408889634
SIDE = 4
ROWS = 64
VMEM = pltpu.VMEM
NT = (((1,), (1,)), ((), ()))


def place():
    t = lax.axis_index("tensor")
    core = lax.rem(lax.axis_index("rep"), 2)
    y, x = lax.div(t, SIDE), lax.rem(t, SIDE)
    major = y * (1 - core) + x * core
    minor = x * (1 - core) + y * core
    step_major, step_minor = SIDE - (SIDE - 1) * core, 1 + (SIDE - 1) * core

    def device(i, j):
        return lax.rem(i, SIDE) * step_major + lax.rem(j, SIDE) * step_minor

    return y, x, major, minor, device


class Copies:
    def __init__(self, send, recv):
        self.send, self.recv, self.used, self.all = send, recv, 0, []

    def start(self, src, dst, where):
        copy = pltpu.make_async_remote_copy(
            src_ref=src,
            dst_ref=dst,
            send_sem=self.send.at[self.used],
            recv_sem=self.recv.at[self.used],
            device_id=where,
            device_id_type=MESH,
        )
        copy.start()
        self.used += 1
        self.all.append(copy)
        return copy

    def drain(self):
        for copy in self.all:
            copy.wait_send()


def tensor(t):
    return {"tensor": t}


def greet(tensor_peers, rep_peers=()):
    barrier = pltpu.get_barrier_semaphore()
    for t in tensor_peers:
        pl.semaphore_signal(barrier, inc=1, device_id=tensor(t), device_id_type=MESH)
    for r in rep_peers:
        pl.semaphore_signal(barrier, inc=1, device_id={"rep": r}, device_id_type=MESH)
    pl.semaphore_wait(barrier, len(tensor_peers) + len(rep_peers))


class Gather:
    def __init__(self, copies, at):
        y, x, self.a, self.b, self.device = place()
        self.copies, self.at = copies, at

    def go(self, i, j, ti, tj):
        return self.copies.start(self.at(i, j), self.at(i, j), tensor(self.device(ti, tj)))

    def begin(self):
        a, b = self.a, self.b
        self.right = self.go(a, b, a, b + 1)
        self.left = self.go(a, b, a, b + 3)
        self.up = [self.go(a, b, a + 1, b)]
        self.down = [self.go(a, b, a + 3, b)]

    def spread(self, j):
        a, b = self.a, self.b
        self.up.append(self.go(a, j, a + 1, b))
        self.down.append(self.go(a, j, a + 3, b))

    def half(self, i, j, part):
        return self.at(i, j).at[pl.ds(part * (ROWS // 2), ROWS // 2)]

    def first(self):
        a, b = self.a, self.b
        self.right.wait_recv()
        one = self.half(a, b + 3, 0)
        far_one = self.copies.start(one, one, tensor(self.device(a, b + 1)))
        self.spread(b + 3)
        self.left.wait_recv()
        two = self.half(a, b + 1, 1)
        far_two = self.copies.start(two, two, tensor(self.device(a, b + 3)))
        self.spread(b + 1)
        far_one.wait_recv()
        far_two.wait_recv()
        self.spread(b + 2)

    def middle(self):
        a, b = self.a, self.b
        self.up[0].wait_recv()
        self.far = [self.go(a + 3, b, a + 1, b)]
        self.down[1].wait_recv()
        self.far.append(self.go(a + 1, b + 3, a + 3, b))
        self.down[2].wait_recv()
        self.far.append(self.go(a + 1, b + 1, a + 3, b))
        self.up[3].wait_recv()
        self.far.append(self.go(a + 3, b + 2, a + 1, b))
        self.up[1].wait_recv()
        self.up[2].wait_recv()
        self.down[0].wait_recv()
        self.down[3].wait_recv()

    def last(self):
        for copy in self.far:
            copy.wait_recv()


class Scatter:
    def __init__(self, copies, parts, far, near, row, row_far, row_near):
        y, x, self.a, self.b, self.device = place()
        self.copies, self.parts, self.far, self.near = copies, parts, far, near
        self.row, self.row_far, self.row_near = row, row_far, row_near

    def pair(self, i, half):
        return self.parts.at[lax.rem(i, SIDE), pl.ds(2 * half, 2)]

    def send_far(self):
        a, b = self.a, self.b
        self.up_far = self.copies.start(
            self.pair(a + 2, 0), self.far.at[0], tensor(self.device(a + 1, b))
        )
        self.down_far = self.copies.start(
            self.pair(a + 2, 1), self.far.at[1], tensor(self.device(a + 3, b))
        )

    def send_near(self):
        a, b = self.a, self.b
        self.up_near = self.copies.start(
            self.pair(a + 1, 1), self.near.at[0, pl.ds(2, 2)], tensor(self.device(a + 1, b))
        )
        self.down_near = self.copies.start(
            self.pair(a + 3, 0), self.near.at[1, pl.ds(0, 2)], tensor(self.device(a + 3, b))
        )

    def pass_on(self):
        a, b = self.a, self.b
        self.up_far.wait_recv()
        self.pair(a + 1, 0)[...] = (
            self.pair(a + 1, 0)[...].astype(jnp.float32) + self.far[0].astype(jnp.float32)
        ).astype(jnp.bfloat16)
        self.up_sum = self.copies.start(
            self.pair(a + 1, 0), self.near.at[0, pl.ds(0, 2)], tensor(self.device(a + 1, b))
        )
        self.down_far.wait_recv()
        self.pair(a + 3, 1)[...] = (
            self.pair(a + 3, 1)[...].astype(jnp.float32) + self.far[1].astype(jnp.float32)
        ).astype(jnp.bfloat16)
        self.down_sum = self.copies.start(
            self.pair(a + 3, 1), self.near.at[1, pl.ds(2, 2)], tensor(self.device(a + 3, b))
        )

    def total(self, j):
        at = lax.rem(j, SIDE)
        return (
            self.parts[lax.rem(self.a, SIDE), at].astype(jnp.float32)
            + self.near[0, at].astype(jnp.float32)
            + self.near[1, at].astype(jnp.float32)
        )

    def finish(self):
        a, b = self.a, self.b
        half = ROWS // 2
        for copy in (self.up_near, self.down_near, self.up_sum, self.down_sum):
            copy.wait_recv()
        right, left = tensor(self.device(a, b + 1)), tensor(self.device(a, b + 3))
        top, low = pl.ds(0, half), pl.ds(half, half)

        def row(j):
            return self.row.at[lax.rem(j, SIDE)]

        row(b + 2)[...] = self.total(b + 2).astype(jnp.bfloat16)
        right_far = self.copies.start(row(b + 2).at[top], self.row_far.at[0], right)
        left_far = self.copies.start(row(b + 2).at[low], self.row_far.at[1], left)
        row(b + 1)[...] = self.total(b + 1).astype(jnp.bfloat16)
        right_near = self.copies.start(row(b + 1).at[low], self.row_near.at[0, low], right)
        row(b + 3)[...] = self.total(b + 3).astype(jnp.bfloat16)
        left_near = self.copies.start(row(b + 3).at[top], self.row_near.at[1, top], left)
        own = self.total(b)
        right_far.wait_recv()
        row(b + 1).at[top][...] = (
            row(b + 1).at[top][...].astype(jnp.float32) + self.row_far[0].astype(jnp.float32)
        ).astype(jnp.bfloat16)
        right_sum = self.copies.start(row(b + 1).at[top], self.row_near.at[0, top], right)
        left_far.wait_recv()
        row(b + 3).at[low][...] = (
            row(b + 3).at[low][...].astype(jnp.float32) + self.row_far[1].astype(jnp.float32)
        ).astype(jnp.bfloat16)
        left_sum = self.copies.start(row(b + 3).at[low], self.row_near.at[1, low], left)
        for copy in (right_near, left_near, right_sum, left_sum):
            copy.wait_recv()
        return (
            own + self.row_near[0].astype(jnp.float32) + self.row_near[1].astype(jnp.float32)
        )


class SmallSum:
    def __init__(self, copies, over_x, over_y):
        t = lax.axis_index("tensor")
        self.y, self.x = lax.div(t, SIDE), lax.rem(t, SIDE)
        self.copies, self.over_x, self.over_y = copies, over_x, over_y

    def begin(self, value):
        self.over_x[self.x] = value.astype(jnp.bfloat16)
        mine = self.over_x.at[self.x]
        self.sent = [
            self.copies.start(
                mine, mine, tensor(SIDE * self.y + lax.rem(self.x + k, SIDE))
            )
            for k in (1, 2, 3)
        ]

    def middle(self):
        for copy in self.sent:
            copy.wait_recv()
        self.over_y[self.y] = sum(
            self.over_x[k].astype(jnp.float32) for k in range(SIDE)
        ).astype(jnp.bfloat16)
        mine = self.over_y.at[self.y]
        self.sent = [
            self.copies.start(
                mine, mine, tensor(SIDE * lax.rem(self.y + k, SIDE) + self.x)
            )
            for k in (1, 2, 3)
        ]

    def finish(self):
        for copy in self.sent:
            copy.wait_recv()
        return sum(self.over_y[k].astype(jnp.float32) for k in range(SIDE))


def layer_norm(values, gain_row, shift_row):
    average = jnp.mean(values, axis=-1, keepdims=True)
    centred = values - average
    spread = jnp.mean(centred * centred, axis=-1, keepdims=True)
    return centred * lax.rsqrt(spread + 1e-05) * gain_row + shift_row


def project_kernel(
    reps,
    scale,
    x_ref,
    dec_ref,
    len_ref,
    w_hbm,
    cache_hbm,
    out_ref,
    attn_ref,
    rows,
    w_ref,
    cache_ref,
    states,
    local_sem,
    send_sem,
    recv_sem,
):
    load_w = pltpu.make_async_copy(w_hbm, w_ref, local_sem.at[0])
    load_w.start()
    load_cache = pltpu.make_async_copy(cache_hbm, cache_ref, local_sem.at[1])
    load_cache.start()
    y, x, a, b, device = place()
    rep = lax.axis_index("rep")
    copies = Copies(send_sem, recv_sem)
    rows[device(a, b)] = x_ref[...]
    greet(
        [device(a, b + 1), device(a, b + 3), device(a + 1, b), device(a + 3, b)],
        [lax.rem(rep + k, reps) for k in range(1, reps)],
    )
    gather = Gather(copies, lambda i, j: rows.at[device(i, j)])
    gather.begin()
    load_w.wait()
    dec = (
        lax.dot_general(w_ref[...], dec_ref[...], NT, preferred_element_type=jnp.float32)
        .astype(jnp.bfloat16)
        .astype(jnp.float32)
    )
    gather.first()
    load_cache.wait()
    hd = cache_ref.shape[2] // 2
    heads = cache_ref.shape[1]
    span = cache_ref.shape[3]
    lanes = dec.shape[1]
    lane = lax.broadcasted_iota(jnp.int32, (1, lanes), 1)
    position = rep * span + lax.broadcasted_iota(jnp.int32, (1, span), 1)

    def request(r, state):
        pick = lane == r
        column = jnp.sum(jnp.where(pick, dec, 0.0), axis=1, keepdims=True)
        valid = position < len_ref[r]
        out = []
        for h in range(heads):
            query = column[3 * hd * h : 3 * hd * h + hd]
            key = cache_ref[r, h, :hd].astype(jnp.float32)
            value = cache_ref[r, h, hd:].astype(jnp.float32)
            score = jnp.sum(key * query, axis=0, keepdims=True) * scale
            score = jnp.where(valid, score, NEG)
            high = jnp.max(score, axis=1, keepdims=True)
            weight = jnp.where(valid, jnp.exp(score - high), 0.0)
            total = jnp.sum(weight, axis=1, keepdims=True)
            mixed = jnp.sum(value * weight, axis=1, keepdims=True)
            highs, totals, mixes = state[h]
            out.append(
                (
                    jnp.where(pick, high, highs),
                    jnp.where(pick, total, totals),
                    jnp.where(pick, mixed, mixes),
                )
            )
        return tuple(out)

    empty = tuple(
        (
            jnp.full((1, lanes), NEG, jnp.float32),
            jnp.zeros((1, lanes), jnp.float32),
            jnp.zeros((hd, lanes), jnp.float32),
        )
        for _ in range(heads)
    )
    state = lax.fori_loop(0, cache_ref.shape[0], request, empty)
    for h in range(heads):
        states[rep, h, :hd] = state[h][2]
        states[rep, h, hd : hd + 8] = jnp.broadcast_to(state[h][0], (8, lanes))
        states[rep, h, hd + 8 : hd + 16] = jnp.broadcast_to(state[h][1], (8, lanes))
    sent = [
        copies.start(states.at[rep], states.at[rep], {"rep": lax.rem(rep + k, reps)})
        for k in range(1, reps)
    ]
    gather.middle()
    for copy in sent:
        copy.wait_recv()
    for h in range(heads):
        base = 3 * hd * h
        query, key, value = (dec[base + hd * k : base + hd * (k + 1)] for k in range(3))
        own = jnp.sum(query * key, axis=0, keepdims=True) * scale
        highest = own
        for k in range(reps):
            highest = jnp.maximum(highest, states[k, h, hd : hd + 1])
        own_weight = jnp.exp(own - highest)
        total, mixed = own_weight, own_weight * value
        for k in range(reps):
            factor = jnp.exp(states[k, h, hd : hd + 1] - highest)
            total = total + factor * states[k, h, hd + 8 : hd + 9]
            mixed = mixed + factor * states[k, h, :hd]
        attn_ref[hd * h : hd * (h + 1)] = (mixed / total).astype(attn_ref.dtype)
    gather.last()

    @pl.loop(0, SIDE)
    def _(i):
        block = rows[pl.ds(SIDE * i, SIDE)].reshape(SIDE * ROWS, rows.shape[2])
        out_ref[:, pl.ds(pl.multiple_of(i * SIDE * ROWS, SIDE * ROWS), SIDE * ROWS)] = (
            lax.dot_general(w_ref[...], block, NT, preferred_element_type=jnp.float32).astype(
                out_ref.dtype
            )
        )

    copies.drain()


def attend_kernel(
    scale, offset_ref, first_ref, qkv_ref, kv_ref, seg_row, seg_col, out_ref, q_ref, m_ref, l_ref, acc_ref
):
    head = pl.program_id(0)
    hd = q_ref.shape[1]
    span = seg_row.shape[1]
    block, key_block = 256, 1024
    factor = scale * LOG2E
    q_ref[...] = qkv_ref[0, 0].astype(jnp.float32).T.astype(jnp.bfloat16)
    offset = offset_ref[0]

    def absorb(score, values):
        high = jnp.maximum(m_ref[...], jnp.max(score, axis=1, keepdims=True))
        decay = jnp.exp2((m_ref[...] - high) * factor)
        weight = jnp.exp2((score - high) * factor)
        m_ref[...] = high
        l_ref[...] = l_ref[...] * decay + jnp.sum(weight, axis=1, keepdims=True)
        acc_ref[...] = acc_ref[...] * decay + lax.dot_general(
            weight.astype(jnp.bfloat16), values, NT, preferred_element_type=jnp.float32
        )

    for i in range(span // block):
        rows = slice(i * block, (i + 1) * block)
        m_ref[...] = jnp.full(m_ref.shape, NEG, jnp.float32)
        l_ref[...] = jnp.zeros(l_ref.shape, jnp.float32)
        acc_ref[...] = jnp.zeros(acc_ref.shape, jnp.float32)
        seg_q = seg_col[rows]
        if (i * block) < span // 2:

            @pl.when((first_ref[i] == 0) & (offset > 0))
            def _():
                @pl.loop(0, lax.div(offset + (key_block - 1), key_block))
                def _(j):
                    at = pl.multiple_of(j * key_block, key_block)
                    score = jnp.dot(
                        q_ref[rows],
                        kv_ref[0, :hd, pl.ds(at, key_block)],
                        preferred_element_type=jnp.float32,
                    )
                    where = at + lax.broadcasted_iota(jnp.int32, (1, key_block), 1)
                    absorb(
                        jnp.where(where < offset, score, NEG),
                        kv_ref[0, hd:, pl.ds(at, key_block)],
                    )

                keep = seg_q == 0
                m_ref[...] = jnp.where(keep, m_ref[...], NEG)
                l_ref[...] = jnp.where(keep, l_ref[...], 0.0)
                acc_ref[...] = jnp.where(keep, acc_ref[...], 0.0)

        low = max(0, (i - span // 2 // block) * block)
        high = (i + 1) * block
        score = jnp.dot(
            q_ref[rows], qkv_ref[0, 1, :, low:high], preferred_element_type=jnp.float32
        )
        shape = (block, high - low)
        query_at = i * block + lax.broadcasted_iota(jnp.int32, shape, 0)
        key_at = low + lax.broadcasted_iota(jnp.int32, shape, 1)
        seen = (seg_row[:, low:high] == seg_q) & (key_at <= query_at)
        absorb(jnp.where(seen, score, NEG), qkv_ref[0, 2, :, low:high])
        result = (acc_ref[...] / l_ref[...]).astype(out_ref.dtype)
        for h in range(out_ref.shape[1] // hd):

            @pl.when(head == h)
            def _():
                out_ref[rows, h * hd : (h + 1) * hd] = result


def tail_kernel(
    attn_ref,
    dec_attn_ref,
    x_ref,
    x_dec_ref,
    w_out_ref,
    up_bias_ref,
    biases_ref,
    gains_ref,
    shifts_ref,
    w_up_hbm,
    w_down_hbm,
    w_next_hbm,
    out_ref,
    next_ref,
    dec_out_ref,
    dec_next_ref,
    w_up_ref,
    w_down_ref,
    w_next_ref,
    slabs,
    rows,
    parts,
    more,
    far,
    near,
    row,
    row_far,
    row_near,
    over_x,
    over_y,
    local_sem,
    send_sem,
    recv_sem,
):
    loads = []
    for k, (source, target) in enumerate(
        ((w_up_hbm, w_up_ref), (w_down_hbm, w_down_ref), (w_next_hbm, w_next_ref))
    ):
        loads.append(pltpu.make_async_copy(source, target, local_sem.at[k]))
        loads[-1].start()
    y, x, a, b, device = place()
    copies = Copies(send_sem, recv_sem)
    greet(
        [SIDE * y + lax.rem(x + k, SIDE) for k in (1, 2, 3)]
        + [SIDE * lax.rem(y + k, SIDE) + x for k in (1, 2, 3)]
    )
    width = x_ref.shape[1]
    chunk = (SIDE, ROWS, width)

    dec_sum = SmallSum(copies, over_x.at[0], over_y.at[0])
    dec_sum.begin(
        jnp.dot(dec_attn_ref[...], w_out_ref[...], preferred_element_type=jnp.float32)
    )

    def out_share(i):
        left = jnp.concatenate(
            [
                attn_ref[pl.ds(pl.multiple_of(device(i, j) * ROWS, ROWS), ROWS)]
                for j in range(SIDE)
            ],
            axis=0,
        )
        parts[lax.rem(i, SIDE)] = (
            jnp.dot(left, w_out_ref[...], preferred_element_type=jnp.float32)
            .astype(jnp.bfloat16)
            .reshape(chunk)
        )

    scatter = Scatter(copies, parts, far.at[0], near.at[0], row.at[0], row_far.at[0], row_near.at[0])
    out_share(a + 2)
    scatter.send_far()
    out_share(a + 1)
    out_share(a + 3)
    scatter.send_near()
    out_share(a)
    dec_sum.middle()
    scatter.pass_on()
    dec_first = layer_norm(
        x_dec_ref[...].astype(jnp.float32) + dec_sum.finish() + biases_ref[0:1],
        gains_ref[0:1],
        shifts_ref[0:1],
    ).astype(jnp.bfloat16)
    attn_sum = scatter.finish()
    first = layer_norm(
        x_ref[...].astype(jnp.float32) + attn_sum + biases_ref[0:1], gains_ref[0:1], shifts_ref[0:1]
    ).astype(jnp.bfloat16)

    def slab(i, j):
        return slabs.at[lax.rem(i, SIDE), lax.rem(j, SIDE)]

    slab(a, b)[...] = first
    gather = Gather(copies, slab)
    gather.begin()
    loads[0].wait()
    loads[1].wait()

    def mlp(value):
        inner = jnp.dot(value, w_up_ref[...], preferred_element_type=jnp.float32) + up_bias_ref[...]
        hidden = (0.5 * inner * (1.0 + lax.erf(inner * 0.7071067811865476))).astype(jnp.bfloat16)
        return jnp.dot(hidden, w_down_ref[...], preferred_element_type=jnp.float32)

    dec_sum = SmallSum(copies, over_x.at[1], over_y.at[1])
    dec_sum.begin(mlp(dec_first))

    def mlp_share(i):
        at = lax.rem(i, SIDE)
        more[at] = (
            mlp(slabs[at].reshape(SIDE * ROWS, width)).astype(jnp.bfloat16).reshape(chunk)
        )

    scatter = Scatter(copies, more, far.at[1], near.at[1], row.at[1], row_far.at[1], row_near.at[1])
    gather.first()
    mlp_share(a)
    gather.middle()
    mlp_share(a + 1)
    mlp_share(a + 3)
    scatter.send_near()
    dec_sum.middle()
    gather.last()
    mlp_share(a + 2)
    scatter.send_far()
    dec_out = layer_norm(
        dec_first.astype(jnp.float32) + dec_sum.finish() + biases_ref[1:2],
        gains_ref[1:2],
        shifts_ref[1:2],
    ).astype(jnp.bfloat16)
    dec_out_ref[...] = dec_out
    loads[2].wait()
    dec_next_ref[...] = lax.dot_general(
        dec_out, w_next_ref[...], NT, preferred_element_type=jnp.float32
    ).astype(jnp.bfloat16)
    scatter.pass_on()
    mlp_sum = scatter.finish()
    second = layer_norm(
        first.astype(jnp.float32) + mlp_sum + biases_ref[1:2], gains_ref[1:2], shifts_ref[1:2]
    ).astype(jnp.bfloat16)
    out_ref[...] = second
    rows[device(a, b)] = second
    gather = Gather(copies, lambda i, j: rows.at[device(i, j)])
    gather.begin()
    gather.first()
    gather.middle()
    gather.last()

    @pl.loop(0, SIDE)
    def _(i):
        block = rows[pl.ds(SIDE * i, SIDE)].reshape(SIDE * ROWS, width)
        next_ref[:, pl.ds(pl.multiple_of(i * SIDE * ROWS, SIDE * ROWS), SIDE * ROWS)] = (
            lax.dot_general(
                w_next_ref[...], block, NT, preferred_element_type=jnp.float32
            ).astype(next_ref.dtype)
        )

    copies.drain()


def per_device(
    reps,
    x_pre,
    x_dec,
    prefix_kv,
    cache_kv,
    dec_len,
    offsets,
    segments,
    w_qkv,
    w_out,
    w_up,
    up_bias,
    w_down,
    biases,
    gains,
    shifts,
    w_next,
):
    heads = prefix_kv.shape[2]
    hd = prefix_kv.shape[3] // 2
    span = segments.shape[1]
    width = x_pre.shape[1]
    decodes = x_dec.shape[0]
    columns = w_qkv.shape[1]
    units = w_up.shape[1]
    scale = hd ** (-0.5)
    bf16, f32 = jnp.bfloat16, jnp.float32
    shape = jax.ShapeDtypeStruct
    whole = pl.BlockSpec(memory_space=VMEM)
    scalars = pl.BlockSpec(memory_space=pltpu.SMEM)
    anywhere = pl.BlockSpec(memory_space=pl.ANY)
    group = SIDE * SIDE

    cache_t = cache_kv.transpose(0, 2, 3, 1)
    n_copies = 16 + reps - 1
    qkv_t, dec_attn_t = pl.pallas_call(
        functools.partial(project_kernel, reps, scale),
        out_shape=(shape((columns, span), bf16), shape((heads * hd, 128), bf16)),
        in_specs=[whole, whole, scalars, anywhere, anywhere],
        out_specs=(whole, whole),
        scratch_shapes=[
            VMEM((group, ROWS, width), bf16),
            VMEM((columns, width), bf16),
            VMEM(cache_t.shape, bf16),
            VMEM((reps, heads, hd + 16, 128), f32),
            pltpu.SemaphoreType.DMA((2,)),
            pltpu.SemaphoreType.DMA((n_copies,)),
            pltpu.SemaphoreType.DMA((n_copies,)),
        ],
        compiler_params=pltpu.CompilerParams(
            collective_id=0, has_side_effects=True, vmem_limit_bytes=48 << 20
        ),
        name="project",
    )(x_pre, jnp.pad(x_dec, ((0, 128 - decodes), (0, 0))), dec_len, w_qkv.T, cache_t)

    attn = pl.pallas_call(
        functools.partial(attend_kernel, scale),
        grid=(heads,),
        out_shape=shape((span, heads * hd), bf16),
        in_specs=[
            scalars,
            scalars,
            pl.BlockSpec((1, 3, hd, span), lambda h: (h, 0, 0, 0)),
            pl.BlockSpec((1, 2 * hd, prefix_kv.shape[1]), lambda h: (h, 0, 0)),
            pl.BlockSpec((1, span), lambda h: (0, 0)),
            pl.BlockSpec((span, 1), lambda h: (0, 0)),
        ],
        out_specs=pl.BlockSpec((span, heads * hd), lambda h: (0, 0)),
        scratch_shapes=[
            VMEM((span, hd), bf16),
            VMEM((256, 1), f32),
            VMEM((256, 1), f32),
            VMEM((256, hd), f32),
        ],
        compiler_params=pltpu.CompilerParams(
            dimension_semantics=("arbitrary",), vmem_limit_bytes=48 << 20
        ),
        name="attend",
    )(
        offsets,
        segments[0, :: 256],
        qkv_t.reshape(heads, 3, hd, span),
        prefix_kv[0].transpose(1, 2, 0),
        segments,
        segments.reshape(span, 1),
    )

    n_copies = 2 * (16 + 12 + 6)
    layer_out, next_t, dec_out, dec_next = pl.pallas_call(
        tail_kernel,
        out_shape=(
            shape((ROWS, width), bf16),
            shape((columns, span), bf16),
            shape((decodes, width), bf16),
            shape((decodes, columns), bf16),
        ),
        in_specs=[whole] * 9 + [anywhere] * 3,
        out_specs=(whole,) * 4,
        scratch_shapes=[
            VMEM((width, units), bf16),
            VMEM((units, width), bf16),
            VMEM((columns, width), bf16),
            VMEM((SIDE, SIDE, ROWS, width), bf16),
            VMEM((group, ROWS, width), bf16),
            VMEM((SIDE, SIDE, ROWS, width), bf16),
            VMEM((SIDE, SIDE, ROWS, width), bf16),
            VMEM((2, 2, 2, ROWS, width), bf16),
            VMEM((2, 2, SIDE, ROWS, width), bf16),
            VMEM((2, SIDE, ROWS, width), bf16),
            VMEM((2, 2, ROWS // 2, width), bf16),
            VMEM((2, 2, ROWS, width), bf16),
            VMEM((2, SIDE, decodes, width), bf16),
            VMEM((2, SIDE, decodes, width), bf16),
            pltpu.SemaphoreType.DMA((3,)),
            pltpu.SemaphoreType.DMA((n_copies,)),
            pltpu.SemaphoreType.DMA((n_copies,)),
        ],
        compiler_params=pltpu.CompilerParams(
            collective_id=1, has_side_effects=True, vmem_limit_bytes=60 << 20
        ),
        name="tail",
    )(
        attn,
        dec_attn_t[:, :decodes].T,
        x_pre,
        x_dec,
        w_out,
        up_bias.reshape(1, units),
        biases,
        gains,
        shifts,
        w_up,
        w_down,
        w_next.T,
    )
    return layer_out, next_t.T, dec_out, dec_next


def solution(mesh):
    placed = (
        P(("rep", "tensor"), None),
        P(),
        P("rep", None, "tensor", None),
        P(None, "rep", "tensor", None),
        P(),
        P("rep"),
        P("rep", None),
        P(None, "tensor"),
        P("tensor", None),
        P(None, "tensor"),
        P("tensor"),
        P("tensor", None),
        P(),
        P(),
        P(),
        P(None, "tensor"),
    )
    return jax.shard_map(
        functools.partial(per_device, mesh.shape["rep"]),
        mesh=mesh,
        in_specs=placed,
        out_specs=(P(("rep", "tensor"), None), P("rep", "tensor"), P(), P(None, "tensor")),
        check_vma=False,
    )
```

time: 650 us -> 230 us (0.35)
  waiting for transfers between devices: 411 us -> 0 us
  Pallas kernels: 0 us -> 211 us
  matrix products: 92.5 us -> 0 us
  other arithmetic: 82.2 us -> 0 us
  blocking collectives: 31.6 us -> 0 us
  between operations: 14.4 us -> 1.36 us
    pallas_call x0 -> x3, Pallas kernels: none -> 211 us  [the longest x1 158 us: per_device(): pl.pallas_call(tail_kernel, out_shape=(shape((ROWS, width), bf16), shape(...]
    reduce_scatter x2 -> x0, waiting for transfers between devices: 153 us -> none  [the longest x1 77.8 us: per_device(): lax.psum_scatter(jnp.dot(attn, w_out, preferred_element_type=jnp.float32)...]
    psum x2 -> x0, waiting for transfers between devices: 146 us -> none  [the longest x1 79.6 us: per_device(): lax.psum(jnp.dot(dec_hidden, w_down, preferred_element_type=jnp.float32)....]
    all_gather x3 -> x0, waiting for transfers between devices: 111 us -> none  [the longest x1 57.2 us: per_device(): lax.all_gather(x_pre, 'tensor', axis=0, tiled=True)]
    dot_general x14 -> x0, matrix products: 92.5 us -> none  [the longest x2 22.8 us: attend_block(): jnp.einsum('qhd,khd->hqk', query_rows, keys, preferred_element_type=jnp.f...]
    sub x2 -> x0, other arithmetic: 50.8 us -> none  [attend_block(): weights = jnp.where(mask[None], jnp.exp(scores - highest), 0.0)]
    all_gather x3 -> x0, blocking collectives: 31.6 us -> none  [combined_all(): pieces = jax.tree.map(lambda part: lax.all_gather(part, axis), value)]
    reduce_sum x10 -> x0, other arithmetic: 10.4 us -> none  [the longest x4 4.84 us: layer_norm(): spread = jnp.mean(centred * centred, axis=-1, keepdims=True)]
  transfers between devices with their start and end apart: 7 -> 0, of which waited for: 7 -> 0; matrix products, arithmetic and copies ran while one was open for 9% -> 0% of each run, Pallas kernels for 0% -> 0%
where the time goes in v1:
time: 230 us; the launch traced here: 227 us
  Pallas kernels  211 us (92%)
  local copies, waits for them, and re-layouts  15.5 us (7%)
    pallas_call x1, Pallas kernels, per_device(): pl.pallas_call(tail_kernel, out_shape=(shape((ROWS, width), bf16), shape(...  158 us
    pallas_call x1, Pallas kernels, per_device(): pl.pallas_call(functools.partial(project_kernel, reps, scale), out_shape=...  41.9 us
    unnamed x16, local copies, waits for them, and re-layouts  10.9 us
    pallas_call x1, Pallas kernels, per_device(): pl.pallas_call(functools.partial(attend_kernel, scale), grid=(heads,), ou...  10.3 us

profile of v1, /device:TPU:0, one launch (start us, length us, event | category | flops | bytes accessed | tf_op | source)
XLA Modules:
  0.0 227.4 jit_solution(15769365791501759459)
XLA Ops:
  1.3 0.8 slice.6
  2.1 1.3 reshape.19.up_bias_ref
  3.3 0.9 copy.21.seg_col
  4.2 0.9 pad.4.dec_ref
  5.2 0.0 copy-start.1
  5.2 1.7 copy-done.1
  6.9 0.0 copy-start.3
  6.9 1.0 copy-done.3
  7.8 0.0 copy-start.5
  7.8 0.7 copy-done.5
  8.5 0.0 copy-start
  8.5 0.0 copy-start.4
  8.5 41.9 %project.1 = (bf16[480,1024]{1,0:T(8,128)(2,1)S(1)}, bf16[160,128]{1,0:T(8,128)(2,1)S(1)}) custom-call(bf16[64,2560]{1,0:T(8,128)(2,1)S(1)} %copy-done.3, bf16[128,2560]{1,0:T(8,128)(2,1)S(1)} %pad.4.dec_ref, s32[16]{0:T(128)S(1)} %copy-done.5, bf16[480,2560]{1,0:T(8,128)(2,1)S(1)} %bitcast.13, bf16[16,2,160,512]{3,2,1,0:T(8,128)(2,1)} %bitcast.17), custom_call_target="tpu_custom_call" | custom-call | tf_op jit(solution)/shard_map/project/pallas_call | solution.py:638
  50.4 0.0 copy-done
  50.4 0.0 copy-done.4
  50.4 10.3 %attend.1.attn_ref = bf16[1024,160]{1,0:T(8,128)(2,1)S(1)} custom-call(s32[1]{0:T(128)S(6)} %copy.27.offset_ref, s32[4]{0:T(128)S(1)} %bitcast.16, bf16[2,3,80,1024]{3,2,1,0:T(8,128)(2,1)S(1)} %bitcast.14, bf16[2,160,4096]{2,1,0:T(8,128)(2,1)S(1)} %bitcast.12, s32[1,1024]{1,0:T(1,128)S(1)} %copy-done.4, s32[1024,1]{1,0:T(8,128)S(1)} %copy.21.seg_col), custom_call_target="tpu_custom_call" | custom-call | tf_op jit(solution)/shard_map/attend/pallas_call | solution.py:658
  60.7 0.0 copy-start.2
  60.8 0.8 copy-done.2
  61.5 0.1 copy.22
  61.6 0.6 slice_bitcast_fusion.dec_attn_ref
  62.2 158.4 %tail.1 = (bf16[64,2560]{1,0:T(8,128)(2,1)}, bf16[480,1024]{1,0:T(8,128)(2,1)}, bf16[16,2560]{1,0:T(8,128)(2,1)}, bf16[16,480]{1,0:T(8,128)(2,1)}) custom-call(bf16[1024,160]{1,0:T(8,128)(2,1)} %copy-done.2, bf16[16,160]{1,0:T(8,128)(2,1)} %slice_bitcast_fusion.dec_attn_ref, bf16[64,2560]{1,0:T(8,128)(2,1)} %x_ref.3, bf16[16,2560]{1,0:T(8,128)(2,1)} %x_dec_ref.1, ...), custom_call_target="tpu_custom_call" | custom-call | tf_op jit(solution)/shard_map/tail/pallas_call | solution.py:691
  220.6 1.7 copy.28
  222.3 2.2 copy.29
  224.6 1.5 copy.30
  226.1 1.3 copy.31
Async XLA Ops:
  5.2 1.7 copy-start.1
  6.9 1.0 copy-start.3
  7.8 0.7 copy-start.5
  8.5 41.9 %copy-start = (bf16[1,4096,2,160]{1,3,2,0:T(8,128)(2,1)S(1)}, bf16[1,4096,2,160]{1,3,2,0:T(8,128)(2,1)}, u32[]{:S(2)}) copy-start(bf16[1,4096,2,160]{1,3,2,0:T(8,128)(2,1)} %param.18) | copy-start | bytes 7864324
  8.5 41.9 %copy-start.4 = (s32[1,1024]{1,0:T(1,128)S(1)}, s32[1,1024]{1,0:T(1,128)}, u32[]{:S(2)}) copy-start(s32[1,1024]{1,0:T(1,128)} %seg_row.1) | copy-start | bytes 12292
  60.7 0.8 copy-start.2

commit v2 on v1

--- a/solution.py
+++ b/solution.py
@@ -67,19 +67,21 @@
 
 
 class Gather:
-    def __init__(self, copies, at):
+    def __init__(self, copies, at, own=None):
         y, x, self.a, self.b, self.device = place()
-        self.copies, self.at = copies, at
+        self.copies, self.at, self.own = copies, at, own
 
     def go(self, i, j, ti, tj):
         return self.copies.start(self.at(i, j), self.at(i, j), tensor(self.device(ti, tj)))
 
     def begin(self):
         a, b = self.a, self.b
-        self.right = self.go(a, b, a, b + 1)
-        self.left = self.go(a, b, a, b + 3)
-        self.up = [self.go(a, b, a + 1, b)]
-        self.down = [self.go(a, b, a + 3, b)]
+        own = self.at(a, b) if self.own is None else self.own
+        self.right, self.left, up, down = (
+            self.copies.start(own, self.at(a, b), tensor(self.device(i, j)))
+            for i, j in ((a, b + 1), (a, b + 3), (a + 1, b), (a + 3, b))
+        )
+        self.up, self.down = [up], [down]
 
     def spread(self, j):
         a, b = self.a, self.b
@@ -123,92 +125,143 @@
             copy.wait_recv()
 
 
+class RingSum:
+    def __init__(self, copies, row, far, near, index, to):
+        self.copies, self.slabs, self.far, self.near = copies, row, far, near
+        self.c, self.next, self.prev = index, to(index + 1), to(index + 3)
+        half = ROWS // 2
+        self.top, self.low = pl.ds(0, half), pl.ds(half, half)
+
+    def row(self, k):
+        return self.slabs.at[lax.rem(self.c + k, SIDE)]
+
+    def send_far(self):
+        self.next_far = self.copies.start(self.row(2).at[self.top], self.far.at[0], self.next)
+        self.prev_far = self.copies.start(self.row(2).at[self.low], self.far.at[1], self.prev)
+
+    def send_next(self):
+        self.next_near = self.copies.start(
+            self.row(1).at[self.low], self.near.at[0, self.low], self.next
+        )
+
+    def send_prev(self):
+        self.prev_near = self.copies.start(
+            self.row(3).at[self.top], self.near.at[1, self.top], self.prev
+        )
+
+    def pass_on(self):
+        self.next_far.wait_recv()
+        add_into(self.row(1).at[self.top], self.far[0])
+        self.next_sum = self.copies.start(
+            self.row(1).at[self.top], self.near.at[0, self.top], self.next
+        )
+        self.prev_far.wait_recv()
+        add_into(self.row(3).at[self.low], self.far[1])
+        self.prev_sum = self.copies.start(
+            self.row(3).at[self.low], self.near.at[1, self.low], self.prev
+        )
+
+    def finish(self, own):
+        for copy in (self.next_near, self.prev_near, self.next_sum, self.prev_sum):
+            copy.wait_recv()
+        return own + self.near[0].astype(jnp.float32) + self.near[1].astype(jnp.float32)
+
+
+def add_into(ref, value):
+    ref[...] = (ref[...].astype(jnp.float32) + value.astype(jnp.float32)).astype(ref.dtype)
+
+
 class Scatter:
     def __init__(self, copies, parts, far, near, row, row_far, row_near):
-        y, x, self.a, self.b, self.device = place()
+        y, x, a, b, self.device = place()
+        self.a, self.b = a, b
         self.copies, self.parts, self.far, self.near = copies, parts, far, near
-        self.row, self.row_far, self.row_near = row, row_far, row_near
-
-    def pair(self, i, half):
-        return self.parts.at[lax.rem(i, SIDE), pl.ds(2 * half, 2)]
+        self.ring = RingSum(
+            copies, row, row_far, row_near, b, lambda j: tensor(self.device(a, j))
+        )
+        self.above, self.below = tensor(self.device(a + 1, b)), tensor(self.device(a + 3, b))
+        self.ups, self.downs = (b + 2, b + 1), (b + 3, b)
+
+    def part(self, i, j):
+        return self.parts.at[lax.rem(i, SIDE), lax.rem(j, SIDE)]
+
+    def landing(self, side, j):
+        return self.near.at[side, lax.rem(j, SIDE)]
 
     def send_far(self):
-        a, b = self.a, self.b
-        self.up_far = self.copies.start(
-            self.pair(a + 2, 0), self.far.at[0], tensor(self.device(a + 1, b))
-        )
-        self.down_far = self.copies.start(
-            self.pair(a + 2, 1), self.far.at[1], tensor(self.device(a + 3, b))
-        )
+        self.far_up, self.far_down = [], []
+        for k in range(2):
+            self.far_up.append(
+                self.copies.start(self.part(self.a + 2, self.ups[k]), self.far.at[0, k], self.above)
+            )
+            self.far_down.append(
+                self.copies.start(
+                    self.part(self.a + 2, self.downs[k]), self.far.at[1, k], self.below
+                )
+            )
 
     def send_near(self):
-        a, b = self.a, self.b
-        self.up_near = self.copies.start(
-            self.pair(a + 1, 1), self.near.at[0, pl.ds(2, 2)], tensor(self.device(a + 1, b))
-        )
-        self.down_near = self.copies.start(
-            self.pair(a + 3, 0), self.near.at[1, pl.ds(0, 2)], tensor(self.device(a + 3, b))
-        )
+        self.near_up, self.near_down = [], []
+        for k in range(2):
+            self.near_up.append(
+                self.copies.start(
+                    self.part(self.a + 1, self.downs[k]),
+                    self.landing(0, self.downs[k]),
+                    self.above,
+                )
+            )
+            self.near_down.append(
+                self.copies.start(
+                    self.part(self.a + 3, self.ups[k]), self.landing(1, self.ups[k]), self.below
+                )
+            )
 
     def pass_on(self):
-        a, b = self.a, self.b
-        self.up_far.wait_recv()
-        self.pair(a + 1, 0)[...] = (
-            self.pair(a + 1, 0)[...].astype(jnp.float32) + self.far[0].astype(jnp.float32)
-        ).astype(jnp.bfloat16)
-        self.up_sum = self.copies.start(
-            self.pair(a + 1, 0), self.near.at[0, pl.ds(0, 2)], tensor(self.device(a + 1, b))
-        )
-        self.down_far.wait_recv()
-        self.pair(a + 3, 1)[...] = (
-            self.pair(a + 3, 1)[...].astype(jnp.float32) + self.far[1].astype(jnp.float32)
-        ).astype(jnp.bfloat16)
-        self.down_sum = self.copies.start(
-            self.pair(a + 3, 1), self.near.at[1, pl.ds(2, 2)], tensor(self.device(a + 3, b))
-        )
+        self.sum_up, self.sum_down = [], []
+        for k in range(2):
+            self.far_up[k].wait_recv()
+            add_into(self.part(self.a + 1, self.ups[k]), self.far[0, k])
+            self.sum_up.append(
+                self.copies.start(
+                    self.part(self.a + 1, self.ups[k]), self.landing(0, self.ups[k]), self.above
+                )
+            )
+            self.far_down[k].wait_recv()
+            add_into(self.part(self.a + 3, self.downs[k]), self.far[1, k])
+            self.sum_down.append(
+                self.copies.start(
+                    self.part(self.a + 3, self.downs[k]),
+                    self.landing(1, self.downs[k]),
+                    self.below,
+                )
+            )
 
     def total(self, j):
         at = lax.rem(j, SIDE)
         return (
-            self.parts[lax.rem(self.a, SIDE), at].astype(jnp.float32)
+            self.parts[self.a, at].astype(jnp.float32)
             + self.near[0, at].astype(jnp.float32)
             + self.near[1, at].astype(jnp.float32)
         )
 
     def finish(self):
-        a, b = self.a, self.b
-        half = ROWS // 2
-        for copy in (self.up_near, self.down_near, self.up_sum, self.down_sum):
-            copy.wait_recv()
-        right, left = tensor(self.device(a, b + 1)), tensor(self.device(a, b + 3))
-        top, low = pl.ds(0, half), pl.ds(half, half)
-
-        def row(j):
-            return self.row.at[lax.rem(j, SIDE)]
-
-        row(b + 2)[...] = self.total(b + 2).astype(jnp.bfloat16)
-        right_far = self.copies.start(row(b + 2).at[top], self.row_far.at[0], right)
-        left_far = self.copies.start(row(b + 2).at[low], self.row_far.at[1], left)
-        row(b + 1)[...] = self.total(b + 1).astype(jnp.bfloat16)
-        right_near = self.copies.start(row(b + 1).at[low], self.row_near.at[0, low], right)
-        row(b + 3)[...] = self.total(b + 3).astype(jnp.bfloat16)
-        left_near = self.copies.start(row(b + 3).at[top], self.row_near.at[1, top], left)
-        own = self.total(b)
-        right_far.wait_recv()
-        row(b + 1).at[top][...] = (
-            row(b + 1).at[top][...].astype(jnp.float32) + self.row_far[0].astype(jnp.float32)
-        ).astype(jnp.bfloat16)
-        right_sum = self.copies.start(row(b + 1).at[top], self.row_near.at[0, top], right)
-        left_far.wait_recv()
-        row(b + 3).at[low][...] = (
-            row(b + 3).at[low][...].astype(jnp.float32) + self.row_far[1].astype(jnp.float32)
-        ).astype(jnp.bfloat16)
-        left_sum = self.copies.start(row(b + 3).at[low], self.row_near.at[1, low], left)
-        for copy in (right_near, left_near, right_sum, left_sum):
-            copy.wait_recv()
-        return (
-            own + self.row_near[0].astype(jnp.float32) + self.row_near[1].astype(jnp.float32)
-        )
+        ring, b = self.ring, self.b
+        self.sum_up[0].wait_recv()
+        self.near_down[0].wait_recv()
+        ring.row(2)[...] = self.total(b + 2).astype(jnp.bfloat16)
+        ring.send_far()
+        self.near_up[0].wait_recv()
+        self.sum_down[0].wait_recv()
+        ring.row(3)[...] = self.total(b + 3).astype(jnp.bfloat16)
+        ring.send_prev()
+        self.sum_up[1].wait_recv()
+        self.near_down[1].wait_recv()
+        ring.row(1)[...] = self.total(b + 1).astype(jnp.bfloat16)
+        ring.send_next()
+        ring.pass_on()
+        self.near_up[1].wait_recv()
+        self.sum_down[1].wait_recv()
+        return ring.finish(self.total(b))
 
 
 class SmallSum:
@@ -257,14 +310,17 @@
 def project_kernel(
     reps,
     scale,
-    x_ref,
+    len_ref,
     dec_ref,
-    len_ref,
+    x_hbm,
     w_hbm,
     cache_hbm,
+    w_out_hbm,
     out_ref,
     attn_ref,
+    w_row_hbm,
     rows,
+    dec_rows,
     w_ref,
     cache_ref,
     states,
@@ -272,27 +328,50 @@
     send_sem,
     recv_sem,
 ):
+    y, x, a, b, device = place()
+    load_x = pltpu.make_async_copy(x_hbm, rows.at[device(a, b)], local_sem.at[2])
+    load_x.start()
     load_w = pltpu.make_async_copy(w_hbm, w_ref, local_sem.at[0])
     load_w.start()
     load_cache = pltpu.make_async_copy(cache_hbm, cache_ref, local_sem.at[1])
     load_cache.start()
-    y, x, a, b, device = place()
+    keep_w = pltpu.make_async_copy(w_out_hbm, w_row_hbm.at[b], local_sem.at[3])
+    keep_w.start()
     rep = lax.axis_index("rep")
     copies = Copies(send_sem, recv_sem)
-    rows[device(a, b)] = x_ref[...]
     greet(
-        [device(a, b + 1), device(a, b + 3), device(a + 1, b), device(a + 3, b)],
+        [device(a, b + k) for k in (1, 2, 3)] + [device(a + 1, b), device(a + 3, b)],
         [lax.rem(rep + k, reps) for k in range(1, reps)],
     )
     gather = Gather(copies, lambda i, j: rows.at[device(i, j)])
+    load_x.wait()
     gather.begin()
+    planes = reps // 2
+    quarter = w_out_hbm.shape[1] // planes
+    mine = pl.ds(pl.multiple_of(lax.div(rep, 2) * quarter, 128), quarter)
+    shards = [
+        copies.start(
+            w_out_hbm.at[:, mine], w_row_hbm.at[b, :, mine], tensor(device(a, b + k))
+        )
+        for k in (1, 3, 2)
+    ]
+    dec_rows[...] = jnp.zeros_like(dec_rows)
+    dec_rows[: dec_ref.shape[0]] = dec_ref[...]
     load_w.wait()
     dec = (
-        lax.dot_general(w_ref[...], dec_ref[...], NT, preferred_element_type=jnp.float32)
+        lax.dot_general(w_ref[...], dec_rows[...], NT, preferred_element_type=jnp.float32)
         .astype(jnp.bfloat16)
         .astype(jnp.float32)
     )
     gather.first()
+    spread = []
+    for k, shard in zip((1, 3, 2), shards):
+        shard.wait_recv()
+        piece = w_row_hbm.at[lax.rem(b - k + SIDE, SIDE), :, mine]
+        spread += [
+            copies.start(piece, piece, {"rep": lax.rem(rep + 2 * p, reps)})
+            for p in range(1, planes)
+        ]
     load_cache.wait()
     hd = cache_ref.shape[2] // 2
     heads = cache_ref.shape[1]
@@ -359,7 +438,9 @@
             factor = jnp.exp(states[k, h, hd : hd + 1] - highest)
             total = total + factor * states[k, h, hd + 8 : hd + 9]
             mixed = mixed + factor * states[k, h, :hd]
-        attn_ref[hd * h : hd * (h + 1)] = (mixed / total).astype(attn_ref.dtype)
+        attn_ref[:, hd * h : hd * (h + 1)] = (mixed / total).T[: attn_ref.shape[0]].astype(
+            attn_ref.dtype
+        )
     gather.last()
 
     @pl.loop(0, SIDE)
@@ -371,11 +452,14 @@
             )
         )
 
+    for copy in spread:
+        copy.wait_recv()
+    keep_w.wait()
     copies.drain()
 
 
 def attend_kernel(
-    scale, offset_ref, first_ref, qkv_ref, kv_ref, seg_row, seg_col, out_ref, q_ref, m_ref, l_ref, acc_ref
+    scale, offset_ref, seg_ref, qkv_ref, kv_ref, seg_row, out_ref, q_ref, m_ref, l_ref, acc_ref
 ):
     head = pl.program_id(0)
     hd = q_ref.shape[1]
@@ -384,6 +468,8 @@
     factor = scale * LOG2E
     q_ref[...] = qkv_ref[0, 0].astype(jnp.float32).T.astype(jnp.bfloat16)
     offset = offset_ref[0]
+    seg_keys = seg_row[...].astype(jnp.float32)
+    seg_rows = jnp.broadcast_to(seg_keys, (8, span)).T[:, :1]
 
     def absorb(score, values):
         high = jnp.maximum(m_ref[...], jnp.max(score, axis=1, keepdims=True))
@@ -400,10 +486,10 @@
         m_ref[...] = jnp.full(m_ref.shape, NEG, jnp.float32)
         l_ref[...] = jnp.zeros(l_ref.shape, jnp.float32)
         acc_ref[...] = jnp.zeros(acc_ref.shape, jnp.float32)
-        seg_q = seg_col[rows]
+        seg_q = seg_rows[rows]
         if (i * block) < span // 2:
 
-            @pl.when((first_ref[i] == 0) & (offset > 0))
+            @pl.when((seg_ref[0, i * block] == 0) & (offset > 0))
             def _():
                 @pl.loop(0, lax.div(offset + (key_block - 1), key_block))
                 def _(j):
@@ -432,7 +518,7 @@
         shape = (block, high - low)
         query_at = i * block + lax.broadcasted_iota(jnp.int32, shape, 0)
         key_at = low + lax.broadcasted_iota(jnp.int32, shape, 1)
-        seen = (seg_row[:, low:high] == seg_q) & (key_at <= query_at)
+        seen = (seg_keys[:, low:high] == seg_q) & (key_at <= query_at)
         absorb(jnp.where(seen, score, NEG), qkv_ref[0, 2, :, low:high])
         result = (acc_ref[...] / l_ref[...]).astype(out_ref.dtype)
         for h in range(out_ref.shape[1] // hd):
@@ -443,29 +529,27 @@
 
 
 def tail_kernel(
-    attn_ref,
     dec_attn_ref,
-    x_ref,
     x_dec_ref,
-    w_out_ref,
     up_bias_ref,
     biases_ref,
     gains_ref,
     shifts_ref,
+    attn_hbm,
+    x_hbm,
+    w_row_hbm,
     w_up_hbm,
     w_down_hbm,
-    w_next_hbm,
+    rows,
     out_ref,
-    next_ref,
     dec_out_ref,
-    dec_next_ref,
+    x_ref,
+    w_row_ref,
     w_up_ref,
     w_down_ref,
-    w_next_ref,
+    heads_ref,
     slabs,
-    rows,
     parts,
-    more,
     far,
     near,
     row,
@@ -479,12 +563,22 @@
 ):
     loads = []
     for k, (source, target) in enumerate(
-        ((w_up_hbm, w_up_ref), (w_down_hbm, w_down_ref), (w_next_hbm, w_next_ref))
+        ((w_row_hbm, w_row_ref), (x_hbm, x_ref), (w_up_hbm, w_up_ref), (w_down_hbm, w_down_ref))
     ):
         loads.append(pltpu.make_async_copy(source, target, local_sem.at[k]))
         loads[-1].start()
     y, x, a, b, device = place()
     copies = Copies(send_sem, recv_sem)
+
+    def tokens(i, j):
+        at = pl.multiple_of(device(i, j) * ROWS, ROWS)
+        return attn_hbm.at[pl.ds(at, ROWS)]
+
+    for i in range(SIDE):
+        loads.append(
+            pltpu.make_async_copy(tokens(i, b), heads_ref.at[b, i], local_sem.at[4 + i])
+        )
+        loads[-1].start()
     greet(
         [SIDE * y + lax.rem(x + k, SIDE) for k in (1, 2, 3)]
         + [SIDE * lax.rem(y + k, SIDE) + x for k in (1, 2, 3)]
@@ -492,40 +586,48 @@
     width = x_ref.shape[1]
     chunk = (SIDE, ROWS, width)
 
+    swaps = [
+        copies.start(tokens(i, b + k), heads_ref.at[b, i], tensor(device(a, b + k)))
+        for k in (2, 1, 3)
+        for i in range(SIDE)
+    ]
+    loads[0].wait()
     dec_sum = SmallSum(copies, over_x.at[0], over_y.at[0])
     dec_sum.begin(
-        jnp.dot(dec_attn_ref[...], w_out_ref[...], preferred_element_type=jnp.float32)
+        jnp.dot(dec_attn_ref[...], w_row_ref[b], preferred_element_type=jnp.float32)
     )
-
-    def out_share(i):
-        left = jnp.concatenate(
-            [
-                attn_ref[pl.ds(pl.multiple_of(device(i, j) * ROWS, ROWS), ROWS)]
-                for j in range(SIDE)
-            ],
-            axis=0,
-        )
-        parts[lax.rem(i, SIDE)] = (
-            jnp.dot(left, w_out_ref[...], preferred_element_type=jnp.float32)
-            .astype(jnp.bfloat16)
-            .reshape(chunk)
-        )
-
-    scatter = Scatter(copies, parts, far.at[0], near.at[0], row.at[0], row_far.at[0], row_near.at[0])
-    out_share(a + 2)
-    scatter.send_far()
-    out_share(a + 1)
-    out_share(a + 3)
-    scatter.send_near()
-    out_share(a)
+    for load in loads[4:]:
+        load.wait()
+    for swap in swaps:
+        swap.wait_recv()
+    ring = RingSum(
+        copies, row.at[0], row_far.at[0], row_near.at[0], a, lambda i: tensor(device(i, b))
+    )
+
+    def out_share(k):
+        left = heads_ref[:, lax.rem(a + k, SIDE)]
+        total = sum(
+            jnp.dot(left[j], w_row_ref[j], preferred_element_type=jnp.float32)
+            for j in range(SIDE)
+        )
+        return total
+
+    ring.row(2)[...] = out_share(2).astype(jnp.bfloat16)
+    ring.send_far()
+    ring.row(1)[...] = out_share(1).astype(jnp.bfloat16)
+    ring.send_next()
+    ring.row(3)[...] = out_share(3).astype(jnp.bfloat16)
+    ring.send_prev()
+    ring.pass_on()
     dec_sum.middle()
-    scatter.pass_on()
+    own = out_share(0)
     dec_first = layer_norm(
         x_dec_ref[...].astype(jnp.float32) + dec_sum.finish() + biases_ref[0:1],
         gains_ref[0:1],
         shifts_ref[0:1],
     ).astype(jnp.bfloat16)
-    attn_sum = scatter.finish()
+    loads[1].wait()
+    attn_sum = ring.finish(own)
     first = layer_norm(
         x_ref[...].astype(jnp.float32) + attn_sum + biases_ref[0:1], gains_ref[0:1], shifts_ref[0:1]
     ).astype(jnp.bfloat16)
@@ -536,11 +638,12 @@
     slab(a, b)[...] = first
     gather = Gather(copies, slab)
     gather.begin()
-    loads[0].wait()
-    loads[1].wait()
+    loads[2].wait()
+    loads[3].wait()
 
     def mlp(value):
-        inner = jnp.dot(value, w_up_ref[...], preferred_element_type=jnp.float32) + up_bias_ref[...]
+        inner = jnp.dot(value, w_up_ref[...], preferred_element_type=jnp.float32)
+        inner = inner + up_bias_ref[...][None, :]
         hidden = (0.5 * inner * (1.0 + lax.erf(inner * 0.7071067811865476))).astype(jnp.bfloat16)
         return jnp.dot(hidden, w_down_ref[...], preferred_element_type=jnp.float32)
 
@@ -549,11 +652,11 @@
 
     def mlp_share(i):
         at = lax.rem(i, SIDE)
-        more[at] = (
+        parts[at] = (
             mlp(slabs[at].reshape(SIDE * ROWS, width)).astype(jnp.bfloat16).reshape(chunk)
         )
 
-    scatter = Scatter(copies, more, far.at[1], near.at[1], row.at[1], row_far.at[1], row_near.at[1])
+    scatter = Scatter(copies, parts, far, near, row.at[1], row_far.at[1], row_near.at[1])
     gather.first()
     mlp_share(a)
     gather.middle()
@@ -570,33 +673,36 @@
         shifts_ref[1:2],
     ).astype(jnp.bfloat16)
     dec_out_ref[...] = dec_out
-    loads[2].wait()
-    dec_next_ref[...] = lax.dot_general(
-        dec_out, w_next_ref[...], NT, preferred_element_type=jnp.float32
-    ).astype(jnp.bfloat16)
     scatter.pass_on()
     mlp_sum = scatter.finish()
     second = layer_norm(
         first.astype(jnp.float32) + mlp_sum + biases_ref[1:2], gains_ref[1:2], shifts_ref[1:2]
     ).astype(jnp.bfloat16)
     out_ref[...] = second
-    rows[device(a, b)] = second
-    gather = Gather(copies, lambda i, j: rows.at[device(i, j)])
+    keep = pltpu.make_async_copy(out_ref, rows.at[device(a, b)], local_sem.at[0])
+    keep.start()
+    gather = Gather(copies, lambda i, j: rows.at[device(i, j)], out_ref)
     gather.begin()
     gather.first()
     gather.middle()
     gather.last()
-
-    @pl.loop(0, SIDE)
-    def _(i):
-        block = rows[pl.ds(SIDE * i, SIDE)].reshape(SIDE * ROWS, width)
-        next_ref[:, pl.ds(pl.multiple_of(i * SIDE * ROWS, SIDE * ROWS), SIDE * ROWS)] = (
-            lax.dot_general(
-                w_next_ref[...], block, NT, preferred_element_type=jnp.float32
-            ).astype(next_ref.dtype)
-        )
-
+    keep.wait()
     copies.drain()
+
+
+def next_kernel(rows_ref, own_ref, dec_ref, w_ref, next_ref, out_ref, dec_out_ref, dec_next_ref):
+    block = rows_ref[...].reshape(SIDE * ROWS, rows_ref.shape[2])
+    next_ref[...] = lax.dot_general(
+        w_ref[...], block, NT, preferred_element_type=jnp.float32
+    ).astype(next_ref.dtype)
+
+    @pl.when(pl.program_id(0) == 0)
+    def _():
+        out_ref[...] = own_ref[...]
+        dec_out_ref[...] = dec_ref[...]
+        dec_next_ref[...] = lax.dot_general(
+            dec_ref[...], w_ref[...], NT, preferred_element_type=jnp.float32
+        ).astype(dec_next_ref.dtype)
 
 
 def per_device(
@@ -630,30 +736,36 @@
     shape = jax.ShapeDtypeStruct
     whole = pl.BlockSpec(memory_space=VMEM)
     scalars = pl.BlockSpec(memory_space=pltpu.SMEM)
-    anywhere = pl.BlockSpec(memory_space=pl.ANY)
+    anywhere = pl.BlockSpec(memory_space=pltpu.HBM)
     group = SIDE * SIDE
 
     cache_t = cache_kv.transpose(0, 2, 3, 1)
-    n_copies = 16 + reps - 1
-    qkv_t, dec_attn_t = pl.pallas_call(
+    planes = reps // 2
+    n_copies = 16 + reps - 1 + (SIDE - 1) * planes
+    qkv_t, dec_attn, w_row = pl.pallas_call(
         functools.partial(project_kernel, reps, scale),
-        out_shape=(shape((columns, span), bf16), shape((heads * hd, 128), bf16)),
-        in_specs=[whole, whole, scalars, anywhere, anywhere],
-        out_specs=(whole, whole),
+        out_shape=(
+            shape((columns, span), bf16),
+            shape((decodes, heads * hd), bf16),
+            shape((SIDE,) + w_out.shape, bf16),
+        ),
+        in_specs=[scalars, whole] + [anywhere] * 4,
+        out_specs=(whole, whole, anywhere),
         scratch_shapes=[
             VMEM((group, ROWS, width), bf16),
+            VMEM((128, width), bf16),
             VMEM((columns, width), bf16),
             VMEM(cache_t.shape, bf16),
             VMEM((reps, heads, hd + 16, 128), f32),
-            pltpu.SemaphoreType.DMA((2,)),
+            pltpu.SemaphoreType.DMA((4,)),
             pltpu.SemaphoreType.DMA((n_copies,)),
             pltpu.SemaphoreType.DMA((n_copies,)),
         ],
         compiler_params=pltpu.CompilerParams(
-            collective_id=0, has_side_effects=True, vmem_limit_bytes=48 << 20
+            collective_id=0, has_side_effects=True, vmem_limit_bytes=62 << 20
         ),
         name="project",
-    )(x_pre, jnp.pad(x_dec, ((0, 128 - decodes), (0, 0))), dec_len, w_qkv.T, cache_t)
+    )(dec_len, x_dec, x_pre, w_qkv.T, cache_t, w_out)
 
     attn = pl.pallas_call(
         functools.partial(attend_kernel, scale),
@@ -665,7 +777,6 @@
             pl.BlockSpec((1, 3, hd, span), lambda h: (h, 0, 0, 0)),
             pl.BlockSpec((1, 2 * hd, prefix_kv.shape[1]), lambda h: (h, 0, 0)),
             pl.BlockSpec((1, span), lambda h: (0, 0)),
-            pl.BlockSpec((span, 1), lambda h: (0, 0)),
         ],
         out_specs=pl.BlockSpec((span, heads * hd), lambda h: (0, 0)),
         scratch_shapes=[
@@ -680,40 +791,38 @@
         name="attend",
     )(
         offsets,
-        segments[0, :: 256],
+        segments,
         qkv_t.reshape(heads, 3, hd, span),
         prefix_kv[0].transpose(1, 2, 0),
         segments,
-        segments.reshape(span, 1),
     )
 
-    n_copies = 2 * (16 + 12 + 6)
-    layer_out, next_t, dec_out, dec_next = pl.pallas_call(
+    n_copies = 2 * (16 + 6) + 12 + 12 + 6 + 6
+    rows, own, dec_own = pl.pallas_call(
         tail_kernel,
         out_shape=(
+            shape((group, ROWS, width), bf16),
             shape((ROWS, width), bf16),
-            shape((columns, span), bf16),
             shape((decodes, width), bf16),
-            shape((decodes, columns), bf16),
         ),
-        in_specs=[whole] * 9 + [anywhere] * 3,
-        out_specs=(whole,) * 4,
+        in_specs=[whole] * 6 + [anywhere] * 5,
+        out_specs=(anywhere, whole, whole),
         scratch_shapes=[
+            VMEM((ROWS, width), bf16),
+            VMEM((SIDE,) + w_out.shape, bf16),
             VMEM((width, units), bf16),
             VMEM((units, width), bf16),
-            VMEM((columns, width), bf16),
-            VMEM((SIDE, SIDE, ROWS, width), bf16),
-            VMEM((group, ROWS, width), bf16),
+            VMEM((SIDE, SIDE, ROWS, heads * hd), bf16),
             VMEM((SIDE, SIDE, ROWS, width), bf16),
             VMEM((SIDE, SIDE, ROWS, width), bf16),
-            VMEM((2, 2, 2, ROWS, width), bf16),
-            VMEM((2, 2, SIDE, ROWS, width), bf16),
+            VMEM((2, 2, ROWS, width), bf16),
+            VMEM((2, SIDE, ROWS, width), bf16),
             VMEM((2, SIDE, ROWS, width), bf16),
             VMEM((2, 2, ROWS // 2, width), bf16),
             VMEM((2, 2, ROWS, width), bf16),
             VMEM((2, SIDE, decodes, width), bf16),
             VMEM((2, SIDE, decodes, width), bf16),
-            pltpu.SemaphoreType.DMA((3,)),
+            pltpu.SemaphoreType.DMA((8,)),
             pltpu.SemaphoreType.DMA((n_copies,)),
             pltpu.SemaphoreType.DMA((n_copies,)),
         ],
@@ -722,19 +831,45 @@
         ),
         name="tail",
     )(
-        attn,
-        dec_attn_t[:, :decodes].T,
-        x_pre,
+        dec_attn,
         x_dec,
-        w_out,
-        up_bias.reshape(1, units),
+        up_bias,
         biases,
         gains,
         shifts,
+        attn,
+        x_pre,
+        w_row,
         w_up,
         w_down,
-        w_next.T,
     )
+
+    next_t, layer_out, dec_out, dec_next = pl.pallas_call(
+        next_kernel,
+        grid=(SIDE,),
+        out_shape=(
+            shape((columns, span), bf16),
+            shape((ROWS, width), bf16),
+            shape((decodes, width), bf16),
+            shape((decodes, columns), bf16),
+        ),
+        in_specs=[
+            pl.BlockSpec((SIDE, ROWS, width), lambda i: (i, 0, 0)),
+            pl.BlockSpec((ROWS, width), lambda i: (0, 0)),
+            pl.BlockSpec((decodes, width), lambda i: (0, 0)),
+            pl.BlockSpec((columns, width), lambda i: (0, 0)),
+        ],
+        out_specs=(
+            pl.BlockSpec((columns, SIDE * ROWS), lambda i: (0, i)),
+            pl.BlockSpec((ROWS, width), lambda i: (0, 0)),
+            pl.BlockSpec((decodes, width), lambda i: (0, 0)),
+            pl.BlockSpec((decodes, columns), lambda i: (0, 0)),
+        ),
+        compiler_params=pltpu.CompilerParams(
+            dimension_semantics=("arbitrary",), vmem_limit_bytes=48 << 20
+        ),
+        name="next",
+    )(rows, own, dec_own, w_next.T)
     return layer_out, next_t.T, dec_out, dec_next
 
 

time: 230 us -> 224 us (0.974)
  local copies, waits for them, and re-layouts: 15.5 us -> 5.58 us
  Pallas kernels: 211 us -> 216 us
    pallas_call x1, Pallas kernels: 41.9 us -> 66 us  [per_device(): pl.pallas_call(functools.partial(project_kernel, reps, scale), out_shape=...]
    pallas_call x1 -> x2, Pallas kernels: 158 us -> 137 us  [the longest x1 130 us: per_device(): pl.pallas_call(tail_kernel, out_shape=(shape((group, ROWS, width), bf16),...]
    unnamed x16 -> x14, local copies, waits for them, and re-layouts: 10.9 us -> 5.58 us
    pallas_call x1, Pallas kernels: 10.3 us -> 13.4 us  [per_device(): pl.pallas_call(functools.partial(attend_kernel, scale), grid=(heads,), ou...]
where the time goes in v2:
time: 224 us; the launch traced here: 223 us
  Pallas kernels  216 us (96%)
  local copies, waits for them, and re-layouts  5.58 us (2%)
    pallas_call x1, Pallas kernels, per_device(): pl.pallas_call(tail_kernel, out_shape=(shape((group, ROWS, width), bf16),...  130 us
    pallas_call x1, Pallas kernels, per_device(): pl.pallas_call(functools.partial(project_kernel, reps, scale), out_shape=...  66 us
    pallas_call x1, Pallas kernels, per_device(): pl.pallas_call(functools.partial(attend_kernel, scale), grid=(heads,), ou...  13.4 us
    pallas_call x1, Pallas kernels, per_device(): pl.pallas_call(next_kernel, grid=(SIDE,), out_shape=(shape((columns, span...  6.95 us
    unnamed x14, local copies, waits for them, and re-layouts  5.58 us

profile of v2, /device:TPU:0, one launch (start us, length us, event | category | flops | bytes accessed | tf_op | source)
XLA Modules:
  0.0 223.2 jit_solution(8207770325088900336)
XLA Ops:
  1.3 0.0 copy-start.6
  1.3 66.0 %project.1 = (bf16[480,1024]{1,0:T(8,128)(2,1)}, bf16[16,160]{1,0:T(8,128)(2,1)}, bf16[4,160,2560]{2,1,0:T(8,128)(2,1)}) custom-call(s32[16]{0:T(128)} %len_ref.1, bf16[16,2560]{1,0:T(8,128)(2,1)} %x_dec_ref.1, bf16[64,2560]{1,0:T(8,128)(2,1)} %x_hbm.3, bf16[480,2560]{1,0:T(8,128)(2,1)} %bitcast.12, bf16[16,2,160,512]{3,2,1,0:T(8,128)(2,1)} %bitcast.11, ...), custom_call_target="tpu_custom_call" | custom-call | tf_op jit(solution)/shard_map/project/pallas_call | solution.py:745
  67.2 0.0 copy-done.6
  67.3 0.0 copy-start
  67.3 1.7 copy-done
  69.0 0.0 copy-start.3
  69.0 1.2 copy-done.3
  70.2 13.4 %attend.1.attn_hbm = bf16[1024,160]{1,0:T(8,128)(2,1)S(1)} custom-call(s32[1]{0:T(128)S(6)} %copy.20.offset_ref, s32[1,1024]{1,0:T(1,128)S(1)} %copy-done.6, bf16[2,3,80,1024]{3,2,1,0:T(8,128)(2,1)S(1)} %bitcast.10, bf16[2,160,4096]{2,1,0:T(8,128)(2,1)S(1)} %bitcast.8, s32[1,1024]{1,0:T(1,128)S(1)} %copy-done.6), custom_call_target="tpu_custom_call" | custom-call | tf_op jit(solution)/shard_map/attend/pallas_call | solution.py:770
  83.6 0.0 copy-start.2
  83.7 0.8 copy-done.2
  84.4 0.0 copy-start.1
  84.4 129.9 %tail.1 = (bf16[16,64,2560]{2,1,0:T(8,128)(2,1)}, bf16[64,2560]{1,0:T(8,128)(2,1)}, bf16[16,2560]{1,0:T(8,128)(2,1)}) custom-call(bf16[16,160]{1,0:T(8,128)(2,1)} %get-tuple-element.14.dec_attn_ref, bf16[16,2560]{1,0:T(8,128)(2,1)} %x_dec_ref.1, f32[640]{0:T(1024)} %up_bias_ref.1, f32[2,2560]{1,0:T(2,128)} %biases_ref.1, f32[2,2560]{1,0:T(2,128)} %gains_ref.1, ...), custom_call_target="tpu_custom_call" | custom-call | tf_op jit(solution)/shard_map/tail/pallas_call | solution.py:801
  214.3 0.0 copy-done.1
  214.4 0.0 copy-start.4
  214.4 1.0 copy-done.4
  215.3 0.0 copy-start.5
  215.3 0.9 copy-done.5
  216.2 7.0 %next.1 = (bf16[480,1024]{1,0:T(8,128)(2,1)}, bf16[64,2560]{1,0:T(8,128)(2,1)}, bf16[16,2560]{1,0:T(8,128)(2,1)}, bf16[16,480]{1,0:T(8,128)(2,1)}) custom-call(bf16[16,64,2560]{2,1,0:T(8,128)(2,1)} %get-tuple-element.17.rows_ref, bf16[64,2560]{1,0:T(8,128)(2,1)S(1)} %copy-done.4, bf16[16,2560]{1,0:T(8,128)(2,1)S(1)} %copy-done.5, bf16[480,2560]{1,0:T(8,128)(2,1)S(1)} %bitcast.9), custom_call_target="tpu_custom_call" | custom-call | tf_op jit(solution)/shard_map/next/pallas_call | solution.py:847
Async XLA Ops:
  1.3 66.0 %copy-start.6 = (s32[1,1024]{1,0:T(1,128)S(1)}, s32[1,1024]{1,0:T(1,128)}, u32[]{:S(2)}) copy-start(s32[1,1024]{1,0:T(1,128)} %seg_row.1) | copy-start | bytes 12292
  67.3 1.7 copy-start
  69.0 1.2 copy-start.3
  83.6 0.8 copy-start.2
  84.4 129.9 %copy-start.1 = (bf16[2560,480]{0,1:T(8,128)(2,1)S(1)}, bf16[2560,480]{0,1:T(8,128)(2,1)}, u32[]{:S(2)}) copy-start(bf16[2560,480]{0,1:T(8,128)(2,1)} %param.31) | copy-start | bytes 7372804
  214.4 1.0 copy-start.4
  215.3 0.9 copy-start.5

commit v3 on v2

--- a/solution.py
+++ b/solution.py
@@ -344,8 +344,6 @@
         [lax.rem(rep + k, reps) for k in range(1, reps)],
     )
     gather = Gather(copies, lambda i, j: rows.at[device(i, j)])
-    load_x.wait()
-    gather.begin()
     planes = reps // 2
     quarter = w_out_hbm.shape[1] // planes
     mine = pl.ds(pl.multiple_of(lax.div(rep, 2) * quarter, 128), quarter)
@@ -355,15 +353,10 @@
         )
         for k in (1, 3, 2)
     ]
+    load_x.wait()
+    gather.begin()
     dec_rows[...] = jnp.zeros_like(dec_rows)
     dec_rows[: dec_ref.shape[0]] = dec_ref[...]
-    load_w.wait()
-    dec = (
-        lax.dot_general(w_ref[...], dec_rows[...], NT, preferred_element_type=jnp.float32)
-        .astype(jnp.bfloat16)
-        .astype(jnp.float32)
-    )
-    gather.first()
     spread = []
     for k, shard in zip((1, 3, 2), shards):
         shard.wait_recv()
@@ -372,6 +365,13 @@
             copies.start(piece, piece, {"rep": lax.rem(rep + 2 * p, reps)})
             for p in range(1, planes)
         ]
+    load_w.wait()
+    dec = (
+        lax.dot_general(w_ref[...], dec_rows[...], NT, preferred_element_type=jnp.float32)
+        .astype(jnp.bfloat16)
+        .astype(jnp.float32)
+    )
+    gather.first()
     load_cache.wait()
     hd = cache_ref.shape[2] // 2
     heads = cache_ref.shape[1]
@@ -458,74 +458,95 @@
     copies.drain()
 
 
-def attend_kernel(
-    scale, offset_ref, seg_ref, qkv_ref, kv_ref, seg_row, out_ref, q_ref, m_ref, l_ref, acc_ref
-):
+def attend_kernel(scale, offset_ref, seg_ref, qkv_ref, kv_ref, seg_row, out_ref, q_ref, *state):
     head = pl.program_id(0)
     hd = q_ref.shape[1]
     span = seg_row.shape[1]
     block, key_block = 256, 1024
+    early = span // 2 // block
     factor = scale * LOG2E
     q_ref[...] = qkv_ref[0, 0].astype(jnp.float32).T.astype(jnp.bfloat16)
     offset = offset_ref[0]
     seg_keys = seg_row[...].astype(jnp.float32)
     seg_rows = jnp.broadcast_to(seg_keys, (8, span)).T[:, :1]
-
-    def absorb(score, values):
+    states = [state[3 * i : 3 * i + 3] for i in range(early)]
+
+    def rows(i):
+        return slice(i * block, (i + 1) * block)
+
+    def mix(weight, values):
+        return lax.dot_general(
+            weight.astype(jnp.bfloat16), values, NT, preferred_element_type=jnp.float32
+        )
+
+    def absorb(i, score, values):
+        m_ref, l_ref, acc_ref = states[i]
         high = jnp.maximum(m_ref[...], jnp.max(score, axis=1, keepdims=True))
         decay = jnp.exp2((m_ref[...] - high) * factor)
         weight = jnp.exp2((score - high) * factor)
         m_ref[...] = high
         l_ref[...] = l_ref[...] * decay + jnp.sum(weight, axis=1, keepdims=True)
-        acc_ref[...] = acc_ref[...] * decay + lax.dot_general(
-            weight.astype(jnp.bfloat16), values, NT, preferred_element_type=jnp.float32
-        )
-
-    for i in range(span // block):
-        rows = slice(i * block, (i + 1) * block)
+        acc_ref[...] = acc_ref[...] * decay + mix(weight, values)
+
+    def prefix(count):
+        def step(j, partial):
+            at = pl.multiple_of(j * key_block, key_block)
+            keys = kv_ref[0, :hd, pl.ds(at, key_block)]
+            values = kv_ref[0, hd:, pl.ds(at, key_block)]
+            where = at + lax.broadcasted_iota(jnp.int32, (1, key_block), 1)
+            scores = [
+                jnp.dot(q_ref[rows(i)], keys, preferred_element_type=jnp.float32)
+                for i in range(count)
+            ]
+            for i, score in enumerate(scores):
+                absorb(i, jnp.where(where < offset, score, NEG) if partial else score, values)
+
+        full = lax.div(offset, key_block)
+        pl.loop(0, full)(lambda j: step(j, False))
+        pl.when(full * key_block < offset)(lambda: step(full, True))
+
+    for m_ref, l_ref, acc_ref in states:
         m_ref[...] = jnp.full(m_ref.shape, NEG, jnp.float32)
         l_ref[...] = jnp.zeros(l_ref.shape, jnp.float32)
         acc_ref[...] = jnp.zeros(acc_ref.shape, jnp.float32)
-        seg_q = seg_rows[rows]
-        if (i * block) < span // 2:
-
-            @pl.when((seg_ref[0, i * block] == 0) & (offset > 0))
-            def _():
-                @pl.loop(0, lax.div(offset + (key_block - 1), key_block))
-                def _(j):
-                    at = pl.multiple_of(j * key_block, key_block)
-                    score = jnp.dot(
-                        q_ref[rows],
-                        kv_ref[0, :hd, pl.ds(at, key_block)],
-                        preferred_element_type=jnp.float32,
-                    )
-                    where = at + lax.broadcasted_iota(jnp.int32, (1, key_block), 1)
-                    absorb(
-                        jnp.where(where < offset, score, NEG),
-                        kv_ref[0, hd:, pl.ds(at, key_block)],
-                    )
-
-                keep = seg_q == 0
-                m_ref[...] = jnp.where(keep, m_ref[...], NEG)
-                l_ref[...] = jnp.where(keep, l_ref[...], 0.0)
-                acc_ref[...] = jnp.where(keep, acc_ref[...], 0.0)
-
-        low = max(0, (i - span // 2 // block) * block)
+    seen_to = sum(jnp.where(seg_ref[0, i * block] == 0, 1, 0) for i in range(early))
+    for count in range(1, early + 1):
+        pl.when((seen_to == count) & (offset > 0))(functools.partial(prefix, count))
+
+    results = []
+    for i in range(span // block):
+        low = max(0, (i - early) * block)
         high = (i + 1) * block
+        seg_q = seg_rows[rows(i)]
         score = jnp.dot(
-            q_ref[rows], qkv_ref[0, 1, :, low:high], preferred_element_type=jnp.float32
+            q_ref[rows(i)], qkv_ref[0, 1, :, low:high], preferred_element_type=jnp.float32
         )
         shape = (block, high - low)
         query_at = i * block + lax.broadcasted_iota(jnp.int32, shape, 0)
         key_at = low + lax.broadcasted_iota(jnp.int32, shape, 1)
         seen = (seg_keys[:, low:high] == seg_q) & (key_at <= query_at)
-        absorb(jnp.where(seen, score, NEG), qkv_ref[0, 2, :, low:high])
-        result = (acc_ref[...] / l_ref[...]).astype(out_ref.dtype)
-        for h in range(out_ref.shape[1] // hd):
-
-            @pl.when(head == h)
-            def _():
-                out_ref[rows, h * hd : (h + 1) * hd] = result
+        score = jnp.where(seen, score, NEG)
+        values = qkv_ref[0, 2, :, low:high]
+        peak = jnp.max(score, axis=1, keepdims=True)
+        if i < early:
+            m_ref, l_ref, acc_ref = states[i]
+            keep = seg_q == 0
+            before = jnp.where(keep, m_ref[...], NEG)
+            peak = jnp.maximum(peak, before)
+            decay = jnp.where(keep, jnp.exp2((before - peak) * factor), 0.0)
+        weight = jnp.exp2((score - peak) * factor)
+        total = jnp.sum(weight, axis=1, keepdims=True)
+        mixed = mix(weight, values)
+        if i < early:
+            total = total + l_ref[...] * decay
+            mixed = mixed + acc_ref[...] * decay
+        results.append((mixed / total).astype(out_ref.dtype))
+    for h in range(out_ref.shape[1] // hd):
+
+        @pl.when(head == h)
+        def _():
+            for i, result in enumerate(results):
+                out_ref[rows(i), h * hd : (h + 1) * hd] = result
 
 
 def tail_kernel(
@@ -781,12 +802,10 @@
         out_specs=pl.BlockSpec((span, heads * hd), lambda h: (0, 0)),
         scratch_shapes=[
             VMEM((span, hd), bf16),
-            VMEM((256, 1), f32),
-            VMEM((256, 1), f32),
-            VMEM((256, hd), f32),
+            *([VMEM((256, 1), f32), VMEM((256, 1), f32), VMEM((256, hd), f32)] * 2),
         ],
         compiler_params=pltpu.CompilerParams(
-            dimension_semantics=("arbitrary",), vmem_limit_bytes=48 << 20
+            dimension_semantics=("arbitrary",), vmem_limit_bytes=62 << 20
         ),
         name="attend",
     )(
@@ -866,7 +885,7 @@
             pl.BlockSpec((decodes, columns), lambda i: (0, 0)),
         ),
         compiler_params=pltpu.CompilerParams(
-            dimension_semantics=("arbitrary",), vmem_limit_bytes=48 << 20
+            dimension_semantics=("arbitrary",), vmem_limit_bytes=62 << 20
         ),
         name="next",
     )(rows, own, dec_own, w_next.T)

time: 224 us -> 207 us (0.924)
  Pallas kernels: 216 us -> 205 us
  local copies, waits for them, and re-layouts: 5.58 us -> 0 us
    pallas_call x1, Pallas kernels: 66 us -> 55 us  [per_device(): pl.pallas_call(functools.partial(project_kernel, reps, scale), out_shape=...]
    unnamed x14 -> x0, local copies, waits for them, and re-layouts: 5.58 us -> none
where the time goes in v3:
time: 207 us
  Pallas kernels  205 us (99%)
    pallas_call x1, Pallas kernels, per_device(): pl.pallas_call(tail_kernel, out_shape=(shape((group, ROWS, width), bf16),...  129 us
    pallas_call x1, Pallas kernels, per_device(): pl.pallas_call(functools.partial(project_kernel, reps, scale), out_shape=...  55 us
    pallas_call x1, Pallas kernels, per_device(): pl.pallas_call(functools.partial(attend_kernel, scale), grid=(heads,), ou...  13.4 us
    pallas_call x1, Pallas kernels, per_device(): pl.pallas_call(next_kernel, grid=(SIDE,), out_shape=(shape((columns, span...  7.89 us

profile of v3, /device:TPU:0, one launch (start us, length us, event | category | flops | bytes accessed | tf_op | source)
XLA Modules:
  0.0 206.7 jit_solution(5610954673398523308)
XLA Ops:
  1.3 55.0 %project.1 = (bf16[480,1024]{1,0:T(8,128)(2,1)}, bf16[16,160]{1,0:T(8,128)(2,1)}, bf16[4,160,2560]{2,1,0:T(8,128)(2,1)}) custom-call(s32[16]{0:T(128)} %len_ref.1, bf16[16,2560]{1,0:T(8,128)(2,1)} %x_dec_ref.1, bf16[64,2560]{1,0:T(8,128)(2,1)} %x_hbm.3, bf16[480,2560]{1,0:T(8,128)(2,1)} %bitcast.10, bf16[16,2,160,512]{3,2,1,0:T(8,128)(2,1)} %bitcast.8, ...), custom_call_target="tpu_custom_call" | custom-call | tf_op jit(solution)/shard_map/project/pallas_call | solution.py:766
  56.3 13.4 %attend.1.attn_hbm = bf16[1024,160]{1,0:T(8,128)(2,1)} custom-call(s32[1]{0:T(128)S(6)} %copy.20.offset_ref, s32[1,1024]{1,0:T(1,128)} %seg_row.1, bf16[2,3,80,1024]{3,2,1,0:T(8,128)(2,1)} %bitcast.12, bf16[2,160,4096]{2,1,0:T(8,128)(2,1)} %bitcast.9, s32[1,1024]{1,0:T(1,128)} %seg_row.1), custom_call_target="tpu_custom_call" | custom-call | tf_op jit(solution)/shard_map/attend/pallas_call | solution.py:791
  69.7 129.1 %tail.1 = (bf16[16,64,2560]{2,1,0:T(8,128)(2,1)}, bf16[64,2560]{1,0:T(8,128)(2,1)}, bf16[16,2560]{1,0:T(8,128)(2,1)}) custom-call(bf16[16,160]{1,0:T(8,128)(2,1)} %get-tuple-element.14.dec_attn_ref, bf16[16,2560]{1,0:T(8,128)(2,1)} %x_dec_ref.1, f32[640]{0:T(1024)} %up_bias_ref.1, f32[2,2560]{1,0:T(2,128)} %biases_ref.1, f32[2,2560]{1,0:T(2,128)} %gains_ref.1, ...), custom_call_target="tpu_custom_call" | custom-call | tf_op jit(solution)/shard_map/tail/pallas_call | solution.py:820
  198.8 7.9 %next.1 = (bf16[480,1024]{1,0:T(8,128)(2,1)}, bf16[64,2560]{1,0:T(8,128)(2,1)}, bf16[16,2560]{1,0:T(8,128)(2,1)}, bf16[16,480]{1,0:T(8,128)(2,1)}) custom-call(bf16[16,64,2560]{2,1,0:T(8,128)(2,1)} %get-tuple-element.17.rows_ref, bf16[64,2560]{1,0:T(8,128)(2,1)} %get-tuple-element.18.own_ref, bf16[16,2560]{1,0:T(8,128)(2,1)} %get-tuple-element.19.dec_ref, ...), custom_call_target="tpu_custom_call" | custom-call | tf_op jit(solution)/shard_map/next/pallas_call | solution.py:866

commit v4 on v3

--- a/solution.py
+++ b/solution.py
@@ -165,6 +165,28 @@
         for copy in (self.next_near, self.prev_near, self.next_sum, self.prev_sum):
             copy.wait_recv()
         return own + self.near[0].astype(jnp.float32) + self.near[1].astype(jnp.float32)
+
+
+class RingGather:
+    def __init__(self, copies, slabs, index, to):
+        self.copies, self.slabs, self.c = copies, slabs, index
+        self.next, self.prev = to(index + 1), to(index + 3)
+        half = ROWS // 2
+        self.top, self.low = pl.ds(0, half), pl.ds(half, half)
+
+    def go(self, k, part, where):
+        piece = self.slabs.at[lax.rem(self.c + k, SIDE)].at[part]
+        return self.copies.start(piece, piece, where)
+
+    def run(self):
+        first = (self.go(0, self.top, self.next), self.go(0, self.low, self.prev))
+        second = (self.go(0, self.low, self.next), self.go(0, self.top, self.prev))
+        first[0].wait_recv()
+        far = [self.go(3, self.top, self.next)]
+        first[1].wait_recv()
+        far.append(self.go(1, self.low, self.prev))
+        for copy in (*second, *far):
+            copy.wait_recv()
 
 
 def add_into(ref, value):
@@ -353,10 +375,9 @@
         )
         for k in (1, 3, 2)
     ]
-    load_x.wait()
-    gather.begin()
     dec_rows[...] = jnp.zeros_like(dec_rows)
     dec_rows[: dec_ref.shape[0]] = dec_ref[...]
+    load_x.wait()
     spread = []
     for k, shard in zip((1, 3, 2), shards):
         shard.wait_recv()
@@ -365,6 +386,7 @@
             copies.start(piece, piece, {"rep": lax.rem(rep + 2 * p, reps)})
             for p in range(1, planes)
         ]
+    gather.begin()
     load_w.wait()
     dec = (
         lax.dot_general(w_ref[...], dec_rows[...], NT, preferred_element_type=jnp.float32)
@@ -458,15 +480,13 @@
     copies.drain()
 
 
-def attend_kernel(scale, offset_ref, seg_ref, qkv_ref, kv_ref, seg_row, out_ref, q_ref, *state):
-    head = pl.program_id(0)
+def attend(head, scale, offset, qkv_ref, kv_ref, seg_row, out_ref, q_ref, state):
     hd = q_ref.shape[1]
     span = seg_row.shape[1]
     block, key_block = 256, 1024
     early = span // 2 // block
     factor = scale * LOG2E
-    q_ref[...] = qkv_ref[0, 0].astype(jnp.float32).T.astype(jnp.bfloat16)
-    offset = offset_ref[0]
+    q_ref[...] = qkv_ref[head, 0].astype(jnp.float32).T.astype(jnp.bfloat16)
     seg_keys = seg_row[...].astype(jnp.float32)
     seg_rows = jnp.broadcast_to(seg_keys, (8, span)).T[:, :1]
     states = [state[3 * i : 3 * i + 3] for i in range(early)]
@@ -478,59 +498,48 @@
         return lax.dot_general(
             weight.astype(jnp.bfloat16), values, NT, preferred_element_type=jnp.float32
         )
-
-    def absorb(i, score, values):
-        m_ref, l_ref, acc_ref = states[i]
-        high = jnp.maximum(m_ref[...], jnp.max(score, axis=1, keepdims=True))
-        decay = jnp.exp2((m_ref[...] - high) * factor)
-        weight = jnp.exp2((score - high) * factor)
-        m_ref[...] = high
-        l_ref[...] = l_ref[...] * decay + jnp.sum(weight, axis=1, keepdims=True)
-        acc_ref[...] = acc_ref[...] * decay + mix(weight, values)
-
-    def prefix(count):
-        def step(j, partial):
-            at = pl.multiple_of(j * key_block, key_block)
-            keys = kv_ref[0, :hd, pl.ds(at, key_block)]
-            values = kv_ref[0, hd:, pl.ds(at, key_block)]
-            where = at + lax.broadcasted_iota(jnp.int32, (1, key_block), 1)
-            scores = [
-                jnp.dot(q_ref[rows(i)], keys, preferred_element_type=jnp.float32)
-                for i in range(count)
-            ]
-            for i, score in enumerate(scores):
-                absorb(i, jnp.where(where < offset, score, NEG) if partial else score, values)
-
-        full = lax.div(offset, key_block)
-        pl.loop(0, full)(lambda j: step(j, False))
-        pl.when(full * key_block < offset)(lambda: step(full, True))
 
     for m_ref, l_ref, acc_ref in states:
         m_ref[...] = jnp.full(m_ref.shape, NEG, jnp.float32)
         l_ref[...] = jnp.zeros(l_ref.shape, jnp.float32)
         acc_ref[...] = jnp.zeros(acc_ref.shape, jnp.float32)
-    seen_to = sum(jnp.where(seg_ref[0, i * block] == 0, 1, 0) for i in range(early))
-    for count in range(1, early + 1):
-        pl.when((seen_to == count) & (offset > 0))(functools.partial(prefix, count))
-
-    results = []
+
+    @pl.loop(0, kv_ref.shape[2] // key_block)
+    def _(j):
+        at = pl.multiple_of(j * key_block, key_block)
+        keys = kv_ref[head, :hd, pl.ds(at, key_block)]
+        values = kv_ref[head, hd:, pl.ds(at, key_block)]
+        seen = at + lax.broadcasted_iota(jnp.int32, (1, key_block), 1) < offset
+        scores = [
+            jnp.dot(q_ref[rows(i)], keys, preferred_element_type=jnp.float32)
+            for i in range(early)
+        ]
+        for score, (m_ref, l_ref, acc_ref) in zip(scores, states):
+            score = jnp.where(seen, score, NEG)
+            high = jnp.maximum(m_ref[...], jnp.max(score, axis=1, keepdims=True))
+            decay = jnp.exp2((m_ref[...] - high) * factor)
+            weight = jnp.exp2((score - high) * factor)
+            m_ref[...] = high
+            l_ref[...] = l_ref[...] * decay + jnp.sum(weight, axis=1, keepdims=True)
+            acc_ref[...] = acc_ref[...] * decay + mix(weight, values)
+
     for i in range(span // block):
         low = max(0, (i - early) * block)
         high = (i + 1) * block
         seg_q = seg_rows[rows(i)]
         score = jnp.dot(
-            q_ref[rows(i)], qkv_ref[0, 1, :, low:high], preferred_element_type=jnp.float32
+            q_ref[rows(i)], qkv_ref[head, 1, :, low:high], preferred_element_type=jnp.float32
         )
         shape = (block, high - low)
         query_at = i * block + lax.broadcasted_iota(jnp.int32, shape, 0)
         key_at = low + lax.broadcasted_iota(jnp.int32, shape, 1)
         seen = (seg_keys[:, low:high] == seg_q) & (key_at <= query_at)
         score = jnp.where(seen, score, NEG)
-        values = qkv_ref[0, 2, :, low:high]
+        values = qkv_ref[head, 2, :, low:high]
         peak = jnp.max(score, axis=1, keepdims=True)
         if i < early:
             m_ref, l_ref, acc_ref = states[i]
-            keep = seg_q == 0
+            keep = (seg_q == 0) & (offset > 0)
             before = jnp.where(keep, m_ref[...], NEG)
             peak = jnp.maximum(peak, before)
             decay = jnp.where(keep, jnp.exp2((before - peak) * factor), 0.0)
@@ -540,35 +549,42 @@
         if i < early:
             total = total + l_ref[...] * decay
             mixed = mixed + acc_ref[...] * decay
-        results.append((mixed / total).astype(out_ref.dtype))
-    for h in range(out_ref.shape[1] // hd):
-
-        @pl.when(head == h)
-        def _():
-            for i, result in enumerate(results):
-                out_ref[rows(i), h * hd : (h + 1) * hd] = result
+        out_ref[rows(i), head * hd : (head + 1) * hd] = (mixed / total).astype(out_ref.dtype)
 
 
 def tail_kernel(
+    scale,
+    reps,
+    offset_ref,
+    seg_row,
     dec_attn_ref,
     x_dec_ref,
     up_bias_ref,
     biases_ref,
     gains_ref,
     shifts_ref,
-    attn_hbm,
+    qkv_hbm,
+    kv_hbm,
     x_hbm,
     w_row_hbm,
     w_up_hbm,
     w_down_hbm,
-    rows,
+    w_next_hbm,
+    result_hbm,
     out_ref,
     dec_out_ref,
+    dec_next_ref,
+    qkv_ref,
+    kv_ref,
     x_ref,
     w_row_ref,
     w_up_ref,
     w_down_ref,
+    w_next_ref,
+    attn_ref,
     heads_ref,
+    columns_ref,
+    result_ref,
     slabs,
     parts,
     far,
@@ -578,76 +594,118 @@
     row_near,
     over_x,
     over_y,
+    q_ref,
+    m0_ref,
+    l0_ref,
+    acc0_ref,
+    m1_ref,
+    l1_ref,
+    acc1_ref,
     local_sem,
     send_sem,
     recv_sem,
 ):
+    y, x, a, b, device = place()
     loads = []
     for k, (source, target) in enumerate(
-        ((w_row_hbm, w_row_ref), (x_hbm, x_ref), (w_up_hbm, w_up_ref), (w_down_hbm, w_down_ref))
+        (
+            (qkv_hbm, qkv_ref),
+            (kv_hbm, kv_ref),
+            (w_row_hbm, w_row_ref),
+            (x_hbm, x_ref),
+            (w_next_hbm, w_next_ref.at[b]),
+            (w_up_hbm, w_up_ref),
+            (w_down_hbm, w_down_ref),
+        )
     ):
         loads.append(pltpu.make_async_copy(source, target, local_sem.at[k]))
         loads[-1].start()
-    y, x, a, b, device = place()
+    load_qkv, load_kv, load_row, load_x, load_next, load_up, load_down = loads
     copies = Copies(send_sem, recv_sem)
-
-    def tokens(i, j):
-        at = pl.multiple_of(device(i, j) * ROWS, ROWS)
-        return attn_hbm.at[pl.ds(at, ROWS)]
-
-    for i in range(SIDE):
-        loads.append(
-            pltpu.make_async_copy(tokens(i, b), heads_ref.at[b, i], local_sem.at[4 + i])
-        )
-        loads[-1].start()
+    rep = lax.axis_index("rep")
+    plane, planes = lax.div(rep, 2), reps // 2
+    columns, width = w_next_hbm.shape
+
+    def level(k):
+        return {"rep": lax.rem(rep + 2 * k, reps)}
+
+    def quarter(p):
+        size = width // planes
+        return pl.ds(pl.multiple_of(lax.rem(p, planes) * size, 128), size)
+
     greet(
         [SIDE * y + lax.rem(x + k, SIDE) for k in (1, 2, 3)]
-        + [SIDE * lax.rem(y + k, SIDE) + x for k in (1, 2, 3)]
+        + [SIDE * lax.rem(y + k, SIDE) + x for k in (1, 2, 3)],
+        [lax.rem(rep + 2 * k, reps) for k in (1, planes - 1)],
     )
-    width = x_ref.shape[1]
+    mine = quarter(plane)
+    shards = [
+        copies.start(
+            w_next_hbm.at[:, mine], w_next_ref.at[b, :, mine], tensor(device(a, b + k))
+        )
+        for k in (3, 2, 1)
+    ]
+    attn_ref[...] = jnp.zeros_like(attn_ref)
+    result_ref[...] = jnp.zeros_like(result_ref)
     chunk = (SIDE, ROWS, width)
+    load_row.wait()
+    dec_sum = SmallSum(copies, over_x.at[0], over_y.at[0])
+    dec_sum.begin(
+        jnp.dot(dec_attn_ref[...], w_row_ref[b], preferred_element_type=jnp.float32)
+    )
+    load_qkv.wait()
+    load_kv.wait()
+    state = (m0_ref, l0_ref, acc0_ref, m1_ref, l1_ref, acc1_ref)
+    offset = offset_ref[0]
+    heads = qkv_ref.shape[0]
+    for head in range(heads):
+        attend(head, scale, offset, qkv_ref, kv_ref, seg_row, attn_ref, q_ref, state)
+        if head == 0:
+            dec_sum.middle()
+
+    def tokens(i, j):
+        return attn_ref.at[pl.ds(pl.multiple_of(device(i, j) * ROWS, ROWS), ROWS)]
 
     swaps = [
         copies.start(tokens(i, b + k), heads_ref.at[b, i], tensor(device(a, b + k)))
         for k in (2, 1, 3)
         for i in range(SIDE)
     ]
-    loads[0].wait()
-    dec_sum = SmallSum(copies, over_x.at[0], over_y.at[0])
-    dec_sum.begin(
-        jnp.dot(dec_attn_ref[...], w_row_ref[b], preferred_element_type=jnp.float32)
-    )
-    for load in loads[4:]:
-        load.wait()
+    for i in range(SIDE):
+        heads_ref[b, i] = tokens(i, b)[...]
+    spread = []
+    for k, shard in enumerate(shards):
+        shard.wait_recv()
+        piece = w_next_ref.at[lax.rem(b + 1 + k, SIDE), :, mine]
+        spread += [copies.start(piece, piece, level(p)) for p in (1, planes - 1)]
+    dec_first = layer_norm(
+        x_dec_ref[...].astype(jnp.float32) + dec_sum.finish() + biases_ref[0:1],
+        gains_ref[0:1],
+        shifts_ref[0:1],
+    ).astype(jnp.bfloat16)
     for swap in swaps:
         swap.wait_recv()
     ring = RingSum(
         copies, row.at[0], row_far.at[0], row_near.at[0], a, lambda i: tensor(device(i, b))
     )
-
-    def out_share(k):
-        left = heads_ref[:, lax.rem(a + k, SIDE)]
+    depth = w_row_ref.shape[1]
+    step = width // 5
+    for n in range(0, width, step):
         total = sum(
-            jnp.dot(left[j], w_row_ref[j], preferred_element_type=jnp.float32)
+            jnp.dot(
+                heads_ref[j].reshape(SIDE * ROWS, heads_ref.shape[3])[:, :depth],
+                w_row_ref[j, :, n : n + step],
+                preferred_element_type=jnp.float32,
+            )
             for j in range(SIDE)
         )
-        return total
-
-    ring.row(2)[...] = out_share(2).astype(jnp.bfloat16)
+        row[0, :, :, n : n + step] = total.astype(jnp.bfloat16).reshape(SIDE, ROWS, step)
     ring.send_far()
-    ring.row(1)[...] = out_share(1).astype(jnp.bfloat16)
     ring.send_next()
-    ring.row(3)[...] = out_share(3).astype(jnp.bfloat16)
     ring.send_prev()
     ring.pass_on()
-    dec_sum.middle()
-    own = out_share(0)
-    dec_first = layer_norm(
-        x_dec_ref[...].astype(jnp.float32) + dec_sum.finish() + biases_ref[0:1],
-        gains_ref[0:1],
-        shifts_ref[0:1],
-    ).astype(jnp.bfloat16)
-    loads[1].wait()
+    own = row[0, a].astype(jnp.float32)
+    load_x.wait()
     attn_sum = ring.finish(own)
     first = layer_norm(
         x_ref[...].astype(jnp.float32) + attn_sum + biases_ref[0:1], gains_ref[0:1], shifts_ref[0:1]
@@ -659,8 +717,8 @@
     slab(a, b)[...] = first
     gather = Gather(copies, slab)
     gather.begin()
-    loads[2].wait()
-    loads[3].wait()
+    load_up.wait()
+    load_down.wait()
 
     def mlp(value):
         inner = jnp.dot(value, w_up_ref[...], preferred_element_type=jnp.float32)
@@ -688,42 +746,82 @@
     gather.last()
     mlp_share(a + 2)
     scatter.send_far()
+    passed = []
+    for at, copy in enumerate(spread):
+        copy.wait_recv()
+        j = lax.rem(b + 1 + at // 2, SIDE)
+        go_on, from_plane, part = ((1, planes - 1, 0), (planes - 1, 1, 1))[at % 2]
+        piece = w_next_ref.at[
+            j, pl.ds(part * (columns // 2), columns // 2), quarter(plane + from_plane)
+        ]
+        passed.append(copies.start(piece, piece, level(go_on)))
     dec_out = layer_norm(
         dec_first.astype(jnp.float32) + dec_sum.finish() + biases_ref[1:2],
         gains_ref[1:2],
         shifts_ref[1:2],
     ).astype(jnp.bfloat16)
     dec_out_ref[...] = dec_out
+    load_next.wait()
+    dec_next_ref[...] = lax.dot_general(
+        dec_out, w_next_ref[b], NT, preferred_element_type=jnp.float32
+    ).astype(jnp.bfloat16)
     scatter.pass_on()
     mlp_sum = scatter.finish()
     second = layer_norm(
         first.astype(jnp.float32) + mlp_sum + biases_ref[1:2], gains_ref[1:2], shifts_ref[1:2]
     ).astype(jnp.bfloat16)
     out_ref[...] = second
-    keep = pltpu.make_async_copy(out_ref, rows.at[device(a, b)], local_sem.at[0])
-    keep.start()
-    gather = Gather(copies, lambda i, j: rows.at[device(i, j)], out_ref)
-    gather.begin()
-    gather.first()
-    gather.middle()
-    gather.last()
-    keep.wait()
+    columns_ref[a] = second
+    RingGather(copies, columns_ref, a, lambda i: tensor(device(i, b))).run()
+    for copy in passed:
+        copy.wait_recv()
+    keeps = []
+    for k in (2, 1, 3, 0):
+        j = lax.rem(b + k, SIDE)
+        result_ref[j, :, :, :columns] = (
+            lax.dot_general(
+                columns_ref[...].reshape(SIDE * ROWS, width),
+                w_next_ref[j],
+                NT,
+                preferred_element_type=jnp.float32,
+            )
+            .astype(jnp.bfloat16)
+            .reshape(SIDE, ROWS, columns)
+        )
+        for i in range(SIDE):
+            source, target = result_ref.at[j, i], result_hbm.at[device(i, b)]
+            if k:
+                keeps.append(copies.start(source, target, tensor(device(a, j))))
+            else:
+                local = pltpu.make_async_copy(source, target, local_sem.at[i])
+                local.start()
+                loads.append(local)
+    for copy in keeps:
+        copy.wait_recv()
+    for local in loads[-SIDE:]:
+        local.wait()
     copies.drain()
 
 
-def next_kernel(rows_ref, own_ref, dec_ref, w_ref, next_ref, out_ref, dec_out_ref, dec_next_ref):
-    block = rows_ref[...].reshape(SIDE * ROWS, rows_ref.shape[2])
+def layout_kernel(
+    result_ref, own_ref, dec_ref, dec_result_ref, next_ref, out_ref, dec_out_ref, dec_next_ref
+):
+    columns, lanes = next_ref.shape[0], result_ref.shape[2]
+    same = lax.broadcasted_iota(jnp.int32, (columns, lanes), 0) == lax.broadcasted_iota(
+        jnp.int32, (columns, lanes), 1
+    )
     next_ref[...] = lax.dot_general(
-        w_ref[...], block, NT, preferred_element_type=jnp.float32
+        same.astype(jnp.float32).astype(jnp.bfloat16),
+        result_ref[...].reshape(SIDE * ROWS, lanes),
+        NT,
+        preferred_element_type=jnp.float32,
     ).astype(next_ref.dtype)
 
     @pl.when(pl.program_id(0) == 0)
     def _():
         out_ref[...] = own_ref[...]
         dec_out_ref[...] = dec_ref[...]
-        dec_next_ref[...] = lax.dot_general(
-            dec_ref[...], w_ref[...], NT, preferred_element_type=jnp.float32
-        ).astype(dec_next_ref.dtype)
+        dec_next_ref[...] = dec_result_ref[...]
 
 
 def per_device(
@@ -788,50 +886,30 @@
         name="project",
     )(dec_len, x_dec, x_pre, w_qkv.T, cache_t, w_out)
 
-    attn = pl.pallas_call(
-        functools.partial(attend_kernel, scale),
-        grid=(heads,),
-        out_shape=shape((span, heads * hd), bf16),
-        in_specs=[
-            scalars,
-            scalars,
-            pl.BlockSpec((1, 3, hd, span), lambda h: (h, 0, 0, 0)),
-            pl.BlockSpec((1, 2 * hd, prefix_kv.shape[1]), lambda h: (h, 0, 0)),
-            pl.BlockSpec((1, span), lambda h: (0, 0)),
-        ],
-        out_specs=pl.BlockSpec((span, heads * hd), lambda h: (0, 0)),
-        scratch_shapes=[
-            VMEM((span, hd), bf16),
-            *([VMEM((256, 1), f32), VMEM((256, 1), f32), VMEM((256, hd), f32)] * 2),
-        ],
-        compiler_params=pltpu.CompilerParams(
-            dimension_semantics=("arbitrary",), vmem_limit_bytes=62 << 20
-        ),
-        name="attend",
-    )(
-        offsets,
-        segments,
-        qkv_t.reshape(heads, 3, hd, span),
-        prefix_kv[0].transpose(1, 2, 0),
-        segments,
-    )
-
-    n_copies = 2 * (16 + 6) + 12 + 12 + 6 + 6
-    rows, own, dec_own = pl.pallas_call(
-        tail_kernel,
+    n_copies = 100
+    lanes = 512
+    result, own, dec_own, dec_result = pl.pallas_call(
+        functools.partial(tail_kernel, scale, reps),
         out_shape=(
-            shape((group, ROWS, width), bf16),
+            shape((group, ROWS, lanes), bf16),
             shape((ROWS, width), bf16),
             shape((decodes, width), bf16),
+            shape((decodes, columns), bf16),
         ),
-        in_specs=[whole] * 6 + [anywhere] * 5,
-        out_specs=(anywhere, whole, whole),
+        in_specs=[scalars] + [whole] * 7 + [anywhere] * 7,
+        out_specs=(anywhere, whole, whole, whole),
         scratch_shapes=[
+            VMEM((heads, 3, hd, span), bf16),
+            VMEM((heads, 2 * hd, prefix_kv.shape[1]), bf16),
             VMEM((ROWS, width), bf16),
             VMEM((SIDE,) + w_out.shape, bf16),
             VMEM((width, units), bf16),
             VMEM((units, width), bf16),
-            VMEM((SIDE, SIDE, ROWS, heads * hd), bf16),
+            VMEM((SIDE, columns, width), bf16),
+            VMEM((span, 256), bf16),
+            VMEM((SIDE, SIDE, ROWS, 256), bf16),
+            VMEM((SIDE, ROWS, width), bf16),
+            VMEM((SIDE, SIDE, ROWS, lanes), bf16),
             VMEM((SIDE, SIDE, ROWS, width), bf16),
             VMEM((SIDE, SIDE, ROWS, width), bf16),
             VMEM((2, 2, ROWS, width), bf16),
@@ -841,30 +919,36 @@
             VMEM((2, 2, ROWS, width), bf16),
             VMEM((2, SIDE, decodes, width), bf16),
             VMEM((2, SIDE, decodes, width), bf16),
+            VMEM((span, hd), bf16),
+            *([VMEM((256, 1), f32), VMEM((256, 1), f32), VMEM((256, hd), f32)] * 2),
             pltpu.SemaphoreType.DMA((8,)),
             pltpu.SemaphoreType.DMA((n_copies,)),
             pltpu.SemaphoreType.DMA((n_copies,)),
         ],
         compiler_params=pltpu.CompilerParams(
-            collective_id=1, has_side_effects=True, vmem_limit_bytes=60 << 20
+            collective_id=1, has_side_effects=True, vmem_limit_bytes=62 << 20
         ),
         name="tail",
     )(
+        offsets,
+        segments,
         dec_attn,
         x_dec,
         up_bias,
         biases,
         gains,
         shifts,
-        attn,
+        qkv_t.reshape(heads, 3, hd, span),
+        prefix_kv[0].transpose(1, 2, 0),
         x_pre,
         w_row,
         w_up,
         w_down,
+        w_next.T,
     )
 
     next_t, layer_out, dec_out, dec_next = pl.pallas_call(
-        next_kernel,
+        layout_kernel,
         grid=(SIDE,),
         out_shape=(
             shape((columns, span), bf16),
@@ -873,10 +957,10 @@
             shape((decodes, columns), bf16),
         ),
         in_specs=[
-            pl.BlockSpec((SIDE, ROWS, width), lambda i: (i, 0, 0)),
+            pl.BlockSpec((SIDE, ROWS, lanes), lambda i: (i, 0, 0)),
             pl.BlockSpec((ROWS, width), lambda i: (0, 0)),
             pl.BlockSpec((decodes, width), lambda i: (0, 0)),
-            pl.BlockSpec((columns, width), lambda i: (0, 0)),
+            pl.BlockSpec((decodes, columns), lambda i: (0, 0)),
         ],
         out_specs=(
             pl.BlockSpec((columns, SIDE * ROWS), lambda i: (0, i)),
@@ -887,8 +971,8 @@
         compiler_params=pltpu.CompilerParams(
             dimension_semantics=("arbitrary",), vmem_limit_bytes=62 << 20
         ),
-        name="next",
-    )(rows, own, dec_own, w_next.T)
+        name="layout",
+    )(result, own, dec_own, dec_result)
     return layer_out, next_t.T, dec_out, dec_next
 
 

time: 207 us -> 207 us (level)
    pallas_call x3 -> x2, Pallas kernels: 150 us -> 151 us  [the longest x1 147 us: per_device(): pl.pallas_call(functools.partial(tail_kernel, scale, reps), out_shape=(sh...]
where the time goes in v4:
time: 207 us; the launch traced here: 206 us
  Pallas kernels  205 us (99%)
    pallas_call x1, Pallas kernels, per_device(): pl.pallas_call(functools.partial(tail_kernel, scale, reps), out_shape=(sh...  147 us
    pallas_call x1, Pallas kernels, per_device(): pl.pallas_call(functools.partial(project_kernel, reps, scale), out_shape=...  53.9 us
    pallas_call x1, Pallas kernels, per_device(): pl.pallas_call(layout_kernel, grid=(SIDE,), out_shape=(shape((columns, sp...  4.28 us

profile of v4, /device:TPU:0, one launch (start us, length us, event | category | flops | bytes accessed | tf_op | source)
XLA Modules:
  0.0 206.2 jit_solution(6976332459558071284)
XLA Ops:
  1.3 53.9 %project.1 = (bf16[480,1024]{1,0:T(8,128)(2,1)}, bf16[16,160]{1,0:T(8,128)(2,1)}, bf16[4,160,2560]{2,1,0:T(8,128)(2,1)}) custom-call(s32[16]{0:T(128)} %len_ref.1, bf16[16,2560]{1,0:T(8,128)(2,1)} %x_dec_ref.1, bf16[64,2560]{1,0:T(8,128)(2,1)} %x_hbm.3, bf16[480,2560]{1,0:T(8,128)(2,1)} %bitcast.10, bf16[16,2,160,512]{3,2,1,0:T(8,128)(2,1)} %bitcast.8, ...), custom_call_target="tpu_custom_call" | custom-call | tf_op jit(solution)/shard_map/project/pallas_call | solution.py:864
  55.2 146.8 %tail.1 = (bf16[16,64,512]{2,1,0:T(8,128)(2,1)}, bf16[64,2560]{1,0:T(8,128)(2,1)}, bf16[16,2560]{1,0:T(8,128)(2,1)}, bf16[16,480]{1,0:T(8,128)(2,1)}) custom-call(s32[1]{0:T(128)S(6)} %copy.20.offset_ref, s32[1,1024]{1,0:T(1,128)} %seg_row.1, bf16[16,160]{1,0:T(8,128)(2,1)} %get-tuple-element.15.dec_attn_ref, bf16[16,2560]{1,0:T(8,128)(2,1)} %x_dec_ref.1, ...), custom_call_target="tpu_custom_call" | custom-call | tf_op jit(solution)/shard_map/tail/pallas_call | solution.py:891
  202.0 4.3 %layout.1 = (bf16[480,1024]{1,0:T(8,128)(2,1)}, bf16[64,2560]{1,0:T(8,128)(2,1)}, bf16[16,2560]{1,0:T(8,128)(2,1)}, bf16[16,480]{1,0:T(8,128)(2,1)}) custom-call(bf16[16,64,512]{2,1,0:T(8,128)(2,1)} %get-tuple-element.18.result_ref, bf16[64,2560]{1,0:T(8,128)(2,1)} %get-tuple-element.19.own_ref, bf16[16,2560]{1,0:T(8,128)(2,1)} %get-tuple-element.20.dec_ref, ...), custom_call_target="tpu_custom_call" | custom-call | tf_op jit(solution)/shard_map/layout/pallas_call | solution.py:950

commit v5 on v4

--- a/solution.py
+++ b/solution.py
@@ -186,6 +186,73 @@
         first[1].wait_recv()
         far.append(self.go(1, self.low, self.prev))
         for copy in (*second, *far):
+            copy.wait_recv()
+
+
+def quarter(width, plane, planes):
+    size = width // planes
+    return pl.ds(pl.multiple_of(lax.rem(plane, planes) * size, 128), size)
+
+
+class Levels:
+    def __init__(self, copies, rep, reps):
+        self.copies, self.plane, self.planes = copies, lax.div(rep, 2), reps // 2
+        self.above, self.below = (
+            {"rep": lax.rem(rep + 2 * k, reps)} for k in (1, self.planes - 1)
+        )
+        self.sent = []
+
+    def share(self, array, k):
+        return array.at[:, quarter(array.shape[1], self.plane + k, self.planes)]
+
+    def spread(self, array):
+        piece = self.share(array, 0)
+        self.sent.append(
+            (
+                array,
+                self.copies.start(piece, piece, self.above),
+                self.copies.start(piece, piece, self.below),
+            )
+        )
+
+    def pass_on(self):
+        self.far = []
+        for array, from_below, from_above in self.sent:
+            half = array.shape[0] // 2
+            from_below.wait_recv()
+            piece = self.share(array, self.planes - 1).at[pl.ds(0, half)]
+            self.far.append(self.copies.start(piece, piece, self.above))
+            from_above.wait_recv()
+            piece = self.share(array, 1).at[pl.ds(half, half)]
+            self.far.append(self.copies.start(piece, piece, self.below))
+
+    def finish(self):
+        for copy in self.far:
+            copy.wait_recv()
+
+
+class RowRing:
+    def __init__(self, copies, shards, own, columns, index, to):
+        self.copies, self.shards, self.columns, self.c = copies, shards, columns, index
+        self.next, self.prev = to(index + 1), to(index + 3)
+        half = own.shape[0] // 2
+        self.parts = pl.ds(0, half), pl.ds(half, half)
+        top, low = (own.at[part, columns] for part in self.parts)
+        self.first = (self.go(0, 0, self.next, top), self.go(0, 1, self.prev, low))
+        self.second = (self.go(0, 1, self.next, low), self.go(0, 0, self.prev, top))
+
+    def go(self, k, part, where, source=None):
+        piece = self.shards.at[lax.rem(self.c + k, SIDE), self.parts[part], self.columns]
+        return self.copies.start(piece if source is None else source, piece, where)
+
+    def pass_on(self):
+        self.first[0].wait_recv()
+        self.far = [self.go(3, 0, self.next)]
+        self.first[1].wait_recv()
+        self.far.append(self.go(1, 1, self.prev))
+
+    def finish(self):
+        for copy in (*self.second, *self.far):
             copy.wait_recv()
 
 
@@ -366,27 +433,17 @@
         [lax.rem(rep + k, reps) for k in range(1, reps)],
     )
     gather = Gather(copies, lambda i, j: rows.at[device(i, j)])
-    planes = reps // 2
-    quarter = w_out_hbm.shape[1] // planes
-    mine = pl.ds(pl.multiple_of(lax.div(rep, 2) * quarter, 128), quarter)
+    mine = quarter(w_out_hbm.shape[1], lax.div(rep, 2), reps // 2)
     shards = [
         copies.start(
             w_out_hbm.at[:, mine], w_row_hbm.at[b, :, mine], tensor(device(a, b + k))
         )
         for k in (1, 3, 2)
     ]
+    load_x.wait()
+    gather.begin()
     dec_rows[...] = jnp.zeros_like(dec_rows)
     dec_rows[: dec_ref.shape[0]] = dec_ref[...]
-    load_x.wait()
-    spread = []
-    for k, shard in zip((1, 3, 2), shards):
-        shard.wait_recv()
-        piece = w_row_hbm.at[lax.rem(b - k + SIDE, SIDE), :, mine]
-        spread += [
-            copies.start(piece, piece, {"rep": lax.rem(rep + 2 * p, reps)})
-            for p in range(1, planes)
-        ]
-    gather.begin()
     load_w.wait()
     dec = (
         lax.dot_general(w_ref[...], dec_rows[...], NT, preferred_element_type=jnp.float32)
@@ -394,6 +451,10 @@
         .astype(jnp.float32)
     )
     gather.first()
+    levels = Levels(copies, rep, reps)
+    for k, shard in zip((1, 3, 2), shards):
+        shard.wait_recv()
+        levels.spread(w_row_hbm.at[lax.rem(b - k + SIDE, SIDE)])
     load_cache.wait()
     hd = cache_ref.shape[2] // 2
     heads = cache_ref.shape[1]
@@ -445,6 +506,7 @@
         for k in range(1, reps)
     ]
     gather.middle()
+    levels.pass_on()
     for copy in sent:
         copy.wait_recv()
     for h in range(heads):
@@ -474,8 +536,7 @@
             )
         )
 
-    for copy in spread:
-        copy.wait_recv()
+    levels.finish()
     keep_w.wait()
     copies.drain()
 
@@ -626,33 +687,27 @@
     plane, planes = lax.div(rep, 2), reps // 2
     columns, width = w_next_hbm.shape
 
-    def level(k):
-        return {"rep": lax.rem(rep + 2 * k, reps)}
-
-    def quarter(p):
-        size = width // planes
-        return pl.ds(pl.multiple_of(lax.rem(p, planes) * size, 128), size)
-
     greet(
         [SIDE * y + lax.rem(x + k, SIDE) for k in (1, 2, 3)]
         + [SIDE * lax.rem(y + k, SIDE) + x for k in (1, 2, 3)],
         [lax.rem(rep + 2 * k, reps) for k in (1, planes - 1)],
     )
-    mine = quarter(plane)
-    shards = [
-        copies.start(
-            w_next_hbm.at[:, mine], w_next_ref.at[b, :, mine], tensor(device(a, b + k))
-        )
-        for k in (3, 2, 1)
-    ]
-    attn_ref[...] = jnp.zeros_like(attn_ref)
-    result_ref[...] = jnp.zeros_like(result_ref)
     chunk = (SIDE, ROWS, width)
     load_row.wait()
     dec_sum = SmallSum(copies, over_x.at[0], over_y.at[0])
     dec_sum.begin(
         jnp.dot(dec_attn_ref[...], w_row_ref[b], preferred_element_type=jnp.float32)
     )
+    shards = RowRing(
+        copies,
+        w_next_ref,
+        w_next_hbm,
+        quarter(width, plane, planes),
+        b,
+        lambda j: tensor(device(a, j)),
+    )
+    attn_ref[...] = jnp.zeros_like(attn_ref)
+    result_ref[...] = jnp.zeros_like(result_ref)
     load_qkv.wait()
     load_kv.wait()
     state = (m0_ref, l0_ref, acc0_ref, m1_ref, l1_ref, acc1_ref)
@@ -662,6 +717,7 @@
         attend(head, scale, offset, qkv_ref, kv_ref, seg_row, attn_ref, q_ref, state)
         if head == 0:
             dec_sum.middle()
+            shards.pass_on()
 
     def tokens(i, j):
         return attn_ref.at[pl.ds(pl.multiple_of(device(i, j) * ROWS, ROWS), ROWS)]
@@ -673,16 +729,6 @@
     ]
     for i in range(SIDE):
         heads_ref[b, i] = tokens(i, b)[...]
-    spread = []
-    for k, shard in enumerate(shards):
-        shard.wait_recv()
-        piece = w_next_ref.at[lax.rem(b + 1 + k, SIDE), :, mine]
-        spread += [copies.start(piece, piece, level(p)) for p in (1, planes - 1)]
-    dec_first = layer_norm(
-        x_dec_ref[...].astype(jnp.float32) + dec_sum.finish() + biases_ref[0:1],
-        gains_ref[0:1],
-        shifts_ref[0:1],
-    ).astype(jnp.bfloat16)
     for swap in swaps:
         swap.wait_recv()
     ring = RingSum(
@@ -704,6 +750,15 @@
     ring.send_next()
     ring.send_prev()
     ring.pass_on()
+    shards.finish()
+    levels = Levels(copies, rep, reps)
+    for k in (1, 2, 3):
+        levels.spread(w_next_ref.at[lax.rem(b + k, SIDE)])
+    dec_first = layer_norm(
+        x_dec_ref[...].astype(jnp.float32) + dec_sum.finish() + biases_ref[0:1],
+        gains_ref[0:1],
+        shifts_ref[0:1],
+    ).astype(jnp.bfloat16)
     own = row[0, a].astype(jnp.float32)
     load_x.wait()
     attn_sum = ring.finish(own)
@@ -746,15 +801,8 @@
     gather.last()
     mlp_share(a + 2)
     scatter.send_far()
-    passed = []
-    for at, copy in enumerate(spread):
-        copy.wait_recv()
-        j = lax.rem(b + 1 + at // 2, SIDE)
-        go_on, from_plane, part = ((1, planes - 1, 0), (planes - 1, 1, 1))[at % 2]
-        piece = w_next_ref.at[
-            j, pl.ds(part * (columns // 2), columns // 2), quarter(plane + from_plane)
-        ]
-        passed.append(copies.start(piece, piece, level(go_on)))
+    scatter.pass_on()
+    levels.pass_on()
     dec_out = layer_norm(
         dec_first.astype(jnp.float32) + dec_sum.finish() + biases_ref[1:2],
         gains_ref[1:2],
@@ -765,7 +813,6 @@
     dec_next_ref[...] = lax.dot_general(
         dec_out, w_next_ref[b], NT, preferred_element_type=jnp.float32
     ).astype(jnp.bfloat16)
-    scatter.pass_on()
     mlp_sum = scatter.finish()
     second = layer_norm(
         first.astype(jnp.float32) + mlp_sum + biases_ref[1:2], gains_ref[1:2], shifts_ref[1:2]
@@ -773,8 +820,7 @@
     out_ref[...] = second
     columns_ref[a] = second
     RingGather(copies, columns_ref, a, lambda i: tensor(device(i, b))).run()
-    for copy in passed:
-        copy.wait_recv()
+    levels.finish()
     keeps = []
     for k in (2, 1, 3, 0):
         j = lax.rem(b + k, SIDE)
@@ -859,8 +905,7 @@
     group = SIDE * SIDE
 
     cache_t = cache_kv.transpose(0, 2, 3, 1)
-    planes = reps // 2
-    n_copies = 16 + reps - 1 + (SIDE - 1) * planes
+    n_copies = 16 + reps - 1 + (SIDE - 1) * 5
     qkv_t, dec_attn, w_row = pl.pallas_call(
         functools.partial(project_kernel, reps, scale),
         out_shape=(

time: 207 us -> 201 us (0.971)
  Pallas kernels: 205 us -> 199 us
    pallas_call x1, Pallas kernels: 147 us -> 136 us  [per_device(): pl.pallas_call(functools.partial(tail_kernel, scale, reps), out_shape=(sh...]
    pallas_call x1, Pallas kernels: 53.9 us -> 58.5 us  [per_device(): pl.pallas_call(functools.partial(project_kernel, reps, scale), out_shape=...]
where the time goes in v5:
time: 201 us; the launch traced here: 200 us
  Pallas kernels  199 us (99%)
    pallas_call x1, Pallas kernels, per_device(): pl.pallas_call(functools.partial(tail_kernel, scale, reps), out_shape=(sh...  136 us
    pallas_call x1, Pallas kernels, per_device(): pl.pallas_call(functools.partial(project_kernel, reps, scale), out_shape=...  58.5 us
    pallas_call x1, Pallas kernels, per_device(): pl.pallas_call(layout_kernel, grid=(SIDE,), out_shape=(shape((columns, sp...  4.28 us

profile of v5, /device:TPU:0, one launch (start us, length us, event | category | flops | bytes accessed | tf_op | source)
XLA Modules:
  0.0 200.0 jit_solution(837018191002018841)
XLA Ops:
  1.3 58.5 %project.1 = (bf16[480,1024]{1,0:T(8,128)(2,1)}, bf16[16,160]{1,0:T(8,128)(2,1)}, bf16[4,160,2560]{2,1,0:T(8,128)(2,1)}) custom-call(s32[16]{0:T(128)} %len_ref.1, bf16[16,2560]{1,0:T(8,128)(2,1)} %x_dec_ref.1, bf16[64,2560]{1,0:T(8,128)(2,1)} %x_hbm.3, bf16[480,2560]{1,0:T(8,128)(2,1)} %bitcast.10, bf16[16,2,160,512]{3,2,1,0:T(8,128)(2,1)} %bitcast.8, ...), custom_call_target="tpu_custom_call" | custom-call | tf_op jit(solution)/shard_map/project/pallas_call | solution.py:909
  59.8 135.9 %tail.1 = (bf16[16,64,512]{2,1,0:T(8,128)(2,1)}, bf16[64,2560]{1,0:T(8,128)(2,1)}, bf16[16,2560]{1,0:T(8,128)(2,1)}, bf16[16,480]{1,0:T(8,128)(2,1)}) custom-call(s32[1]{0:T(128)S(6)} %copy.20.offset_ref, s32[1,1024]{1,0:T(1,128)} %seg_row.1, bf16[16,160]{1,0:T(8,128)(2,1)} %get-tuple-element.15.dec_attn_ref, bf16[16,2560]{1,0:T(8,128)(2,1)} %x_dec_ref.1, ...), custom_call_target="tpu_custom_call" | custom-call | tf_op jit(solution)/shard_map/tail/pallas_call | solution.py:936
  195.7 4.3 %layout.1 = (bf16[480,1024]{1,0:T(8,128)(2,1)}, bf16[64,2560]{1,0:T(8,128)(2,1)}, bf16[16,2560]{1,0:T(8,128)(2,1)}, bf16[16,480]{1,0:T(8,128)(2,1)}) custom-call(bf16[16,64,512]{2,1,0:T(8,128)(2,1)} %get-tuple-element.18.result_ref, bf16[64,2560]{1,0:T(8,128)(2,1)} %get-tuple-element.19.own_ref, bf16[16,2560]{1,0:T(8,128)(2,1)} %get-tuple-element.20.dec_ref, ...), custom_call_target="tpu_custom_call" | custom-call | tf_op jit(solution)/shard_map/layout/pallas_call | solution.py:995

commit v6 on v5

--- a/solution.py
+++ b/solution.py
@@ -440,10 +440,14 @@
         )
         for k in (1, 3, 2)
     ]
-    load_x.wait()
-    gather.begin()
     dec_rows[...] = jnp.zeros_like(dec_rows)
     dec_rows[: dec_ref.shape[0]] = dec_ref[...]
+    load_x.wait()
+    levels = Levels(copies, rep, reps)
+    for k, shard in zip((1, 3, 2), shards):
+        shard.wait_recv()
+        levels.spread(w_row_hbm.at[lax.rem(b - k + SIDE, SIDE)])
+    gather.begin()
     load_w.wait()
     dec = (
         lax.dot_general(w_ref[...], dec_rows[...], NT, preferred_element_type=jnp.float32)
@@ -451,10 +455,6 @@
         .astype(jnp.float32)
     )
     gather.first()
-    levels = Levels(copies, rep, reps)
-    for k, shard in zip((1, 3, 2), shards):
-        shard.wait_recv()
-        levels.spread(w_row_hbm.at[lax.rem(b - k + SIDE, SIDE)])
     load_cache.wait()
     hd = cache_ref.shape[2] // 2
     heads = cache_ref.shape[1]
@@ -505,8 +505,8 @@
         copies.start(states.at[rep], states.at[rep], {"rep": lax.rem(rep + k, reps)})
         for k in range(1, reps)
     ]
+    levels.pass_on()
     gather.middle()
-    levels.pass_on()
     for copy in sent:
         copy.wait_recv()
     for h in range(heads):
@@ -793,11 +793,11 @@
     scatter = Scatter(copies, parts, far, near, row.at[1], row_far.at[1], row_near.at[1])
     gather.first()
     mlp_share(a)
+    dec_sum.middle()
     gather.middle()
     mlp_share(a + 1)
     mlp_share(a + 3)
     scatter.send_near()
-    dec_sum.middle()
     gather.last()
     mlp_share(a + 2)
     scatter.send_far()

time: 201 us -> 194 us (0.965)
  Pallas kernels: 199 us -> 192 us
    pallas_call x1, Pallas kernels: 58.5 us -> 51.2 us  [per_device(): pl.pallas_call(functools.partial(project_kernel, reps, scale), out_shape=...]
where the time goes in v6:
time: 194 us; the launch traced here: 193 us
  Pallas kernels  192 us (99%)
    pallas_call x1, Pallas kernels, per_device(): pl.pallas_call(functools.partial(tail_kernel, scale, reps), out_shape=(sh...  136 us
    pallas_call x1, Pallas kernels, per_device(): pl.pallas_call(functools.partial(project_kernel, reps, scale), out_shape=...  51.2 us
    pallas_call x1, Pallas kernels, per_device(): pl.pallas_call(layout_kernel, grid=(SIDE,), out_shape=(shape((columns, sp...  4.27 us

profile of v6, /device:TPU:0, one launch (start us, length us, event | category | flops | bytes accessed | tf_op | source)
XLA Modules:
  0.0 193.0 jit_solution(1273490425257545265)
XLA Ops:
  1.3 51.2 %project.1 = (bf16[480,1024]{1,0:T(8,128)(2,1)}, bf16[16,160]{1,0:T(8,128)(2,1)}, bf16[4,160,2560]{2,1,0:T(8,128)(2,1)}) custom-call(s32[16]{0:T(128)} %len_ref.1, bf16[16,2560]{1,0:T(8,128)(2,1)} %x_dec_ref.1, bf16[64,2560]{1,0:T(8,128)(2,1)} %x_hbm.3, bf16[480,2560]{1,0:T(8,128)(2,1)} %bitcast.10, bf16[16,2,160,512]{3,2,1,0:T(8,128)(2,1)} %bitcast.8, ...), custom_call_target="tpu_custom_call" | custom-call | tf_op jit(solution)/shard_map/project/pallas_call | solution.py:909
  52.5 136.2 %tail.1 = (bf16[16,64,512]{2,1,0:T(8,128)(2,1)}, bf16[64,2560]{1,0:T(8,128)(2,1)}, bf16[16,2560]{1,0:T(8,128)(2,1)}, bf16[16,480]{1,0:T(8,128)(2,1)}) custom-call(s32[1]{0:T(128)S(6)} %copy.20.offset_ref, s32[1,1024]{1,0:T(1,128)} %seg_row.1, bf16[16,160]{1,0:T(8,128)(2,1)} %get-tuple-element.15.dec_attn_ref, bf16[16,2560]{1,0:T(8,128)(2,1)} %x_dec_ref.1, ...), custom_call_target="tpu_custom_call" | custom-call | tf_op jit(solution)/shard_map/tail/pallas_call | solution.py:936
  188.7 4.3 %layout.1 = (bf16[480,1024]{1,0:T(8,128)(2,1)}, bf16[64,2560]{1,0:T(8,128)(2,1)}, bf16[16,2560]{1,0:T(8,128)(2,1)}, bf16[16,480]{1,0:T(8,128)(2,1)}) custom-call(bf16[16,64,512]{2,1,0:T(8,128)(2,1)} %get-tuple-element.18.result_ref, bf16[64,2560]{1,0:T(8,128)(2,1)} %get-tuple-element.19.own_ref, bf16[16,2560]{1,0:T(8,128)(2,1)} %get-tuple-element.20.dec_ref, ...), custom_call_target="tpu_custom_call" | custom-call | tf_op jit(solution)/shard_map/layout/pallas_call | solution.py:995

commit v7 on v6

--- a/solution.py
+++ b/solution.py
@@ -507,6 +507,27 @@
     ]
     levels.pass_on()
     gather.middle()
+
+    def tiles(start):
+        core = lax.rem(rep, 2)
+        for k in (0, 2):
+            at = []
+            for n in (k, k + 1):
+                row_at = (1 - core) * lax.rem(a + start + n // 2, SIDE) + core * n
+                side = (1 - core) * (n % 2) + core * lax.rem(lax.div(a, 2) + start // 2, 2)
+                at.append(2 * row_at + side)
+            block = jnp.concatenate(
+                [rows[pl.ds(2 * t, 2)].reshape(2 * ROWS, rows.shape[2]) for t in at], axis=0
+            )
+            result = lax.dot_general(
+                w_ref[...], block, NT, preferred_element_type=jnp.float32
+            ).astype(out_ref.dtype)
+            for n, t in enumerate(at):
+                out_ref[:, pl.ds(pl.multiple_of(t * 2 * ROWS, 2 * ROWS), 2 * ROWS)] = result[
+                    :, n * 2 * ROWS : (n + 1) * 2 * ROWS
+                ]
+
+    tiles(0)
     for copy in sent:
         copy.wait_recv()
     for h in range(heads):
@@ -526,16 +547,7 @@
             attn_ref.dtype
         )
     gather.last()
-
-    @pl.loop(0, SIDE)
-    def _(i):
-        block = rows[pl.ds(SIDE * i, SIDE)].reshape(SIDE * ROWS, rows.shape[2])
-        out_ref[:, pl.ds(pl.multiple_of(i * SIDE * ROWS, SIDE * ROWS), SIDE * ROWS)] = (
-            lax.dot_general(w_ref[...], block, NT, preferred_element_type=jnp.float32).astype(
-                out_ref.dtype
-            )
-        )
-
+    tiles(2)
     levels.finish()
     keep_w.wait()
     copies.drain()
@@ -550,19 +562,22 @@
     q_ref[...] = qkv_ref[head, 0].astype(jnp.float32).T.astype(jnp.bfloat16)
     seg_keys = seg_row[...].astype(jnp.float32)
     seg_rows = jnp.broadcast_to(seg_keys, (8, span)).T[:, :1]
-    states = [state[3 * i : 3 * i + 3] for i in range(early)]
+    states = [state[2 * i : 2 * i + 2] for i in range(early)]
 
     def rows(i):
         return slice(i * block, (i + 1) * block)
 
     def mix(weight, values):
+        ones = jnp.ones((16, values.shape[1]), jnp.bfloat16)
         return lax.dot_general(
-            weight.astype(jnp.bfloat16), values, NT, preferred_element_type=jnp.float32
-        )
-
-    for m_ref, l_ref, acc_ref in states:
+            weight.astype(jnp.bfloat16),
+            jnp.concatenate([values, ones], axis=0),
+            NT,
+            preferred_element_type=jnp.float32,
+        )
+
+    for m_ref, acc_ref in states:
         m_ref[...] = jnp.full(m_ref.shape, NEG, jnp.float32)
-        l_ref[...] = jnp.zeros(l_ref.shape, jnp.float32)
         acc_ref[...] = jnp.zeros(acc_ref.shape, jnp.float32)
 
     @pl.loop(0, kv_ref.shape[2] // key_block)
@@ -575,13 +590,12 @@
             jnp.dot(q_ref[rows(i)], keys, preferred_element_type=jnp.float32)
             for i in range(early)
         ]
-        for score, (m_ref, l_ref, acc_ref) in zip(scores, states):
+        for score, (m_ref, acc_ref) in zip(scores, states):
             score = jnp.where(seen, score, NEG)
             high = jnp.maximum(m_ref[...], jnp.max(score, axis=1, keepdims=True))
             decay = jnp.exp2((m_ref[...] - high) * factor)
             weight = jnp.exp2((score - high) * factor)
             m_ref[...] = high
-            l_ref[...] = l_ref[...] * decay + jnp.sum(weight, axis=1, keepdims=True)
             acc_ref[...] = acc_ref[...] * decay + mix(weight, values)
 
     for i in range(span // block):
@@ -599,18 +613,18 @@
         values = qkv_ref[head, 2, :, low:high]
         peak = jnp.max(score, axis=1, keepdims=True)
         if i < early:
-            m_ref, l_ref, acc_ref = states[i]
+            m_ref, acc_ref = states[i]
             keep = (seg_q == 0) & (offset > 0)
             before = jnp.where(keep, m_ref[...], NEG)
             peak = jnp.maximum(peak, before)
             decay = jnp.where(keep, jnp.exp2((before - peak) * factor), 0.0)
         weight = jnp.exp2((score - peak) * factor)
-        total = jnp.sum(weight, axis=1, keepdims=True)
         mixed = mix(weight, values)
         if i < early:
-            total = total + l_ref[...] * decay
             mixed = mixed + acc_ref[...] * decay
-        out_ref[rows(i), head * hd : (head + 1) * hd] = (mixed / total).astype(out_ref.dtype)
+        out_ref[rows(i), head * hd : (head + 1) * hd] = (
+            mixed[:, :hd] / mixed[:, hd : hd + 1]
+        ).astype(out_ref.dtype)
 
 
 def tail_kernel(
@@ -657,10 +671,8 @@
     over_y,
     q_ref,
     m0_ref,
-    l0_ref,
     acc0_ref,
     m1_ref,
-    l1_ref,
     acc1_ref,
     local_sem,
     send_sem,
@@ -710,7 +722,7 @@
     result_ref[...] = jnp.zeros_like(result_ref)
     load_qkv.wait()
     load_kv.wait()
-    state = (m0_ref, l0_ref, acc0_ref, m1_ref, l1_ref, acc1_ref)
+    state = (m0_ref, acc0_ref, m1_ref, acc1_ref)
     offset = offset_ref[0]
     heads = qkv_ref.shape[0]
     for head in range(heads):
@@ -781,9 +793,6 @@
         hidden = (0.5 * inner * (1.0 + lax.erf(inner * 0.7071067811865476))).astype(jnp.bfloat16)
         return jnp.dot(hidden, w_down_ref[...], preferred_element_type=jnp.float32)
 
-    dec_sum = SmallSum(copies, over_x.at[1], over_y.at[1])
-    dec_sum.begin(mlp(dec_first))
-
     def mlp_share(i):
         at = lax.rem(i, SIDE)
         parts[at] = (
@@ -793,7 +802,8 @@
     scatter = Scatter(copies, parts, far, near, row.at[1], row_far.at[1], row_near.at[1])
     gather.first()
     mlp_share(a)
-    dec_sum.middle()
+    dec_sum = SmallSum(copies, over_x.at[1], over_y.at[1])
+    dec_sum.begin(mlp(dec_first))
     gather.middle()
     mlp_share(a + 1)
     mlp_share(a + 3)
@@ -803,16 +813,7 @@
     scatter.send_far()
     scatter.pass_on()
     levels.pass_on()
-    dec_out = layer_norm(
-        dec_first.astype(jnp.float32) + dec_sum.finish() + biases_ref[1:2],
-        gains_ref[1:2],
-        shifts_ref[1:2],
-    ).astype(jnp.bfloat16)
-    dec_out_ref[...] = dec_out
-    load_next.wait()
-    dec_next_ref[...] = lax.dot_general(
-        dec_out, w_next_ref[b], NT, preferred_element_type=jnp.float32
-    ).astype(jnp.bfloat16)
+    dec_sum.middle()
     mlp_sum = scatter.finish()
     second = layer_norm(
         first.astype(jnp.float32) + mlp_sum + biases_ref[1:2], gains_ref[1:2], shifts_ref[1:2]
@@ -821,6 +822,7 @@
     columns_ref[a] = second
     RingGather(copies, columns_ref, a, lambda i: tensor(device(i, b))).run()
     levels.finish()
+    load_next.wait()
     keeps = []
     for k in (2, 1, 3, 0):
         j = lax.rem(b + k, SIDE)
@@ -842,6 +844,15 @@
                 local = pltpu.make_async_copy(source, target, local_sem.at[i])
                 local.start()
                 loads.append(local)
+    dec_out = layer_norm(
+        dec_first.astype(jnp.float32) + dec_sum.finish() + biases_ref[1:2],
+        gains_ref[1:2],
+        shifts_ref[1:2],
+    ).astype(jnp.bfloat16)
+    dec_out_ref[...] = dec_out
+    dec_next_ref[...] = lax.dot_general(
+        dec_out, w_next_ref[b], NT, preferred_element_type=jnp.float32
+    ).astype(jnp.bfloat16)
     for copy in keeps:
         copy.wait_recv()
     for local in loads[-SIDE:]:
@@ -965,7 +976,7 @@
             VMEM((2, SIDE, decodes, width), bf16),
             VMEM((2, SIDE, decodes, width), bf16),
             VMEM((span, hd), bf16),
-            *([VMEM((256, 1), f32), VMEM((256, 1), f32), VMEM((256, hd), f32)] * 2),
+            *([VMEM((256, 1), f32), VMEM((256, hd + 16), f32)] * 2),
             pltpu.SemaphoreType.DMA((8,)),
             pltpu.SemaphoreType.DMA((n_copies,)),
             pltpu.SemaphoreType.DMA((n_copies,)),

time: 194 us -> 195 us (level)
  no operation moved by 1% of the time
where the time goes in v7:
time: 195 us; the launch traced here: 193 us
  Pallas kernels  192 us (98%)
    pallas_call x1, Pallas kernels, per_device(): pl.pallas_call(functools.partial(tail_kernel, scale, reps), out_shape=(sh...  138 us
    pallas_call x1, Pallas kernels, per_device(): pl.pallas_call(functools.partial(project_kernel, reps, scale), out_shape=...  49.9 us
    pallas_call x1, Pallas kernels, per_device(): pl.pallas_call(layout_kernel, grid=(SIDE,), out_shape=(shape((columns, sp...  4.27 us

profile of v7, /device:TPU:0, one launch (start us, length us, event | category | flops | bytes accessed | tf_op | source)
XLA Modules:
  0.0 192.9 jit_solution(14486624631607405457)
XLA Ops:
  1.3 49.9 %project.1 = (bf16[480,1024]{1,0:T(8,128)(2,1)}, bf16[16,160]{1,0:T(8,128)(2,1)}, bf16[4,160,2560]{2,1,0:T(8,128)(2,1)}) custom-call(s32[16]{0:T(128)} %len_ref.1, bf16[16,2560]{1,0:T(8,128)(2,1)} %x_dec_ref.1, bf16[64,2560]{1,0:T(8,128)(2,1)} %x_hbm.3, bf16[480,2560]{1,0:T(8,128)(2,1)} %bitcast.10, bf16[16,2,160,512]{3,2,1,0:T(8,128)(2,1)} %bitcast.8, ...), custom_call_target="tpu_custom_call" | custom-call | tf_op jit(solution)/shard_map/project/pallas_call | solution.py:920
  51.1 137.5 %tail.1 = (bf16[16,64,512]{2,1,0:T(8,128)(2,1)}, bf16[64,2560]{1,0:T(8,128)(2,1)}, bf16[16,2560]{1,0:T(8,128)(2,1)}, bf16[16,480]{1,0:T(8,128)(2,1)}) custom-call(s32[1]{0:T(128)S(6)} %copy.20.offset_ref, s32[1,1024]{1,0:T(1,128)} %seg_row.1, bf16[16,160]{1,0:T(8,128)(2,1)} %get-tuple-element.15.dec_attn_ref, bf16[16,2560]{1,0:T(8,128)(2,1)} %x_dec_ref.1, ...), custom_call_target="tpu_custom_call" | custom-call | tf_op jit(solution)/shard_map/tail/pallas_call | solution.py:947
  188.7 4.3 %layout.1 = (bf16[480,1024]{1,0:T(8,128)(2,1)}, bf16[64,2560]{1,0:T(8,128)(2,1)}, bf16[16,2560]{1,0:T(8,128)(2,1)}, bf16[16,480]{1,0:T(8,128)(2,1)}) custom-call(bf16[16,64,512]{2,1,0:T(8,128)(2,1)} %get-tuple-element.18.result_ref, bf16[64,2560]{1,0:T(8,128)(2,1)} %get-tuple-element.19.own_ref, bf16[16,2560]{1,0:T(8,128)(2,1)} %get-tuple-element.20.dec_ref, ...), custom_call_target="tpu_custom_call" | custom-call | tf_op jit(solution)/shard_map/layout/pallas_call | solution.py:1006

commit v8 on v7

--- a/solution.py
+++ b/solution.py
@@ -434,19 +434,17 @@
     )
     gather = Gather(copies, lambda i, j: rows.at[device(i, j)])
     mine = quarter(w_out_hbm.shape[1], lax.div(rep, 2), reps // 2)
-    shards = [
-        copies.start(
-            w_out_hbm.at[:, mine], w_row_hbm.at[b, :, mine], tensor(device(a, b + k))
-        )
-        for k in (1, 3, 2)
-    ]
+    shards = RowRing(
+        copies, w_row_hbm, w_out_hbm, mine, b, lambda j: tensor(device(a, j))
+    )
     dec_rows[...] = jnp.zeros_like(dec_rows)
     dec_rows[: dec_ref.shape[0]] = dec_ref[...]
     load_x.wait()
     levels = Levels(copies, rep, reps)
-    for k, shard in zip((1, 3, 2), shards):
-        shard.wait_recv()
-        levels.spread(w_row_hbm.at[lax.rem(b - k + SIDE, SIDE)])
+    shards.pass_on()
+    shards.finish()
+    for k in (1, 2, 3):
+        levels.spread(w_row_hbm.at[lax.rem(b + k, SIDE)])
     gather.begin()
     load_w.wait()
     dec = (
@@ -811,8 +809,8 @@
     gather.last()
     mlp_share(a + 2)
     scatter.send_far()
+    levels.pass_on()
     scatter.pass_on()
-    levels.pass_on()
     dec_sum.middle()
     mlp_sum = scatter.finish()
     second = layer_norm(
@@ -916,7 +914,7 @@
     group = SIDE * SIDE
 
     cache_t = cache_kv.transpose(0, 2, 3, 1)
-    n_copies = 16 + reps - 1 + (SIDE - 1) * 5
+    n_copies = 16 + reps - 1 + 6 + (SIDE - 1) * 4
     qkv_t, dec_attn, w_row = pl.pallas_call(
         functools.partial(project_kernel, reps, scale),
         out_shape=(

time: 195 us -> 194 us (level)
  Pallas kernels: 192 us -> 189 us
    pallas_call x1, Pallas kernels: 138 us -> 134 us  [per_device(): pl.pallas_call(functools.partial(tail_kernel, scale, reps), out_shape=(sh...]
where the time goes in v8:
time: 194 us; the launch traced here: 190 us
  Pallas kernels  189 us (97%)
    pallas_call x1, Pallas kernels, per_device(): pl.pallas_call(functools.partial(tail_kernel, scale, reps), out_shape=(sh...  134 us
    pallas_call x1, Pallas kernels, per_device(): pl.pallas_call(functools.partial(project_kernel, reps, scale), out_shape=...  51.1 us
    pallas_call x1, Pallas kernels, per_device(): pl.pallas_call(layout_kernel, grid=(SIDE,), out_shape=(shape((columns, sp...  4.27 us

profile of v8, /device:TPU:0, one launch (start us, length us, event | category | flops | bytes accessed | tf_op | source)
XLA Modules:
  0.0 190.2 jit_solution(7782974598694818718)
XLA Ops:
  1.3 51.1 %project.1 = (bf16[480,1024]{1,0:T(8,128)(2,1)}, bf16[16,160]{1,0:T(8,128)(2,1)}, bf16[4,160,2560]{2,1,0:T(8,128)(2,1)}) custom-call(s32[16]{0:T(128)} %len_ref.1, bf16[16,2560]{1,0:T(8,128)(2,1)} %x_dec_ref.1, bf16[64,2560]{1,0:T(8,128)(2,1)} %x_hbm.3, bf16[480,2560]{1,0:T(8,128)(2,1)} %bitcast.10, bf16[16,2,160,512]{3,2,1,0:T(8,128)(2,1)} %bitcast.8, ...), custom_call_target="tpu_custom_call" | custom-call | tf_op jit(solution)/shard_map/project/pallas_call | solution.py:918
  52.4 133.6 %tail.1 = (bf16[16,64,512]{2,1,0:T(8,128)(2,1)}, bf16[64,2560]{1,0:T(8,128)(2,1)}, bf16[16,2560]{1,0:T(8,128)(2,1)}, bf16[16,480]{1,0:T(8,128)(2,1)}) custom-call(s32[1]{0:T(128)S(6)} %copy.20.offset_ref, s32[1,1024]{1,0:T(1,128)} %seg_row.1, bf16[16,160]{1,0:T(8,128)(2,1)} %get-tuple-element.15.dec_attn_ref, bf16[16,2560]{1,0:T(8,128)(2,1)} %x_dec_ref.1, ...), custom_call_target="tpu_custom_call" | custom-call | tf_op jit(solution)/shard_map/tail/pallas_call | solution.py:945
  186.0 4.3 %layout.1 = (bf16[480,1024]{1,0:T(8,128)(2,1)}, bf16[64,2560]{1,0:T(8,128)(2,1)}, bf16[16,2560]{1,0:T(8,128)(2,1)}, bf16[16,480]{1,0:T(8,128)(2,1)}) custom-call(bf16[16,64,512]{2,1,0:T(8,128)(2,1)} %get-tuple-element.18.result_ref, bf16[64,2560]{1,0:T(8,128)(2,1)} %get-tuple-element.19.own_ref, bf16[16,2560]{1,0:T(8,128)(2,1)} %get-tuple-element.20.dec_ref, ...), custom_call_target="tpu_custom_call" | custom-call | tf_op jit(solution)/shard_map/layout/pallas_call | solution.py:1004

commit v9 on v8

--- a/solution.py
+++ b/solution.py
@@ -554,7 +554,7 @@
 def attend(head, scale, offset, qkv_ref, kv_ref, seg_row, out_ref, q_ref, state):
     hd = q_ref.shape[1]
     span = seg_row.shape[1]
-    block, key_block = 256, 1024
+    block, key_block = 256, 2048
     early = span // 2 // block
     factor = scale * LOG2E
     q_ref[...] = qkv_ref[head, 0].astype(jnp.float32).T.astype(jnp.bfloat16)

time: 194 us -> 190 us (0.979)
  Pallas kernels: 189 us -> 186 us
    pallas_call x1, Pallas kernels: 134 us -> 130 us  [per_device(): pl.pallas_call(functools.partial(tail_kernel, scale, reps), out_shape=(sh...]
where the time goes in v9:
time: 190 us; the launch traced here: 187 us
  Pallas kernels  186 us (98%)
    pallas_call x1, Pallas kernels, per_device(): pl.pallas_call(functools.partial(tail_kernel, scale, reps), out_shape=(sh...  130 us
    pallas_call x1, Pallas kernels, per_device(): pl.pallas_call(functools.partial(project_kernel, reps, scale), out_shape=...  51.1 us
    pallas_call x1, Pallas kernels, per_device(): pl.pallas_call(layout_kernel, grid=(SIDE,), out_shape=(shape((columns, sp...  4.27 us

profile of v9, /device:TPU:0, one launch (start us, length us, event | category | flops | bytes accessed | tf_op | source)
XLA Modules:
  0.0 186.8 jit_solution(10925914516630123887)
XLA Ops:
  1.3 51.1 %project.1 = (bf16[480,1024]{1,0:T(8,128)(2,1)}, bf16[16,160]{1,0:T(8,128)(2,1)}, bf16[4,160,2560]{2,1,0:T(8,128)(2,1)}) custom-call(s32[16]{0:T(128)} %len_ref.1, bf16[16,2560]{1,0:T(8,128)(2,1)} %x_dec_ref.1, bf16[64,2560]{1,0:T(8,128)(2,1)} %x_hbm.3, bf16[480,2560]{1,0:T(8,128)(2,1)} %bitcast.10, bf16[16,2,160,512]{3,2,1,0:T(8,128)(2,1)} %bitcast.8, ...), custom_call_target="tpu_custom_call" | custom-call | tf_op jit(solution)/shard_map/project/pallas_call | solution.py:918
  52.4 130.2 %tail.1 = (bf16[16,64,512]{2,1,0:T(8,128)(2,1)}, bf16[64,2560]{1,0:T(8,128)(2,1)}, bf16[16,2560]{1,0:T(8,128)(2,1)}, bf16[16,480]{1,0:T(8,128)(2,1)}) custom-call(s32[1]{0:T(128)S(6)} %copy.20.offset_ref, s32[1,1024]{1,0:T(1,128)} %seg_row.1, bf16[16,160]{1,0:T(8,128)(2,1)} %get-tuple-element.15.dec_attn_ref, bf16[16,2560]{1,0:T(8,128)(2,1)} %x_dec_ref.1, ...), custom_call_target="tpu_custom_call" | custom-call | tf_op jit(solution)/shard_map/tail/pallas_call | solution.py:945
  182.6 4.3 %layout.1 = (bf16[480,1024]{1,0:T(8,128)(2,1)}, bf16[64,2560]{1,0:T(8,128)(2,1)}, bf16[16,2560]{1,0:T(8,128)(2,1)}, bf16[16,480]{1,0:T(8,128)(2,1)}) custom-call(bf16[16,64,512]{2,1,0:T(8,128)(2,1)} %get-tuple-element.18.result_ref, bf16[64,2560]{1,0:T(8,128)(2,1)} %get-tuple-element.19.own_ref, bf16[16,2560]{1,0:T(8,128)(2,1)} %get-tuple-element.20.dec_ref, ...), custom_call_target="tpu_custom_call" | custom-call | tf_op jit(solution)/shard_map/layout/pallas_call | solution.py:1004
